TPU v7x, 32 devices: a whole 2x2x4 slice. The times are simulated.
32 devices in a mesh: rep: 2 (over x), seq: 16 (over z, y, core).
Axes of the slice: x: 2, y: 2, z: 4, core: 2. Of those that a mesh axis runs over, the one named last changes fastest.
Arguments:
- cached_keys: bfloat16 [32768, 1024], P(('rep', 'seq')), parts along dimension 0, may hold values from -6 to 6
- cached_values: bfloat16 [32768, 1024], P(('rep', 'seq')), parts along dimension 0, may hold values from -6 to 6
- window_queries: bfloat16 [256, 8192], P(('rep', 'seq')), parts along dimension 0
- kept_count: int32 [32], P(('rep', 'seq')), parts along dimension 0, may hold values from 1 to 640, 8192 in all
- kept_entry: int32 [20480], P(('rep', 'seq')), parts along dimension 0, may hold values from 0 to 8191
- row_owner: int32 [20480], P(('rep', 'seq')), parts along dimension 0, may hold values from 0 to 15, as said below
Outputs:
- importance: float32 [16, 16384], P('rep', 'seq'), parts along dimension 0
- compact_rows: bfloat16 [20480, 256], P(('rep', 'seq')), parts along dimension 0
- compact_score: bfloat16 [20480], P(('rep', 'seq')), parts along dimension 0
There are 2 independent parts, one for each index of `rep`. A program takes and returns all parts, laid end to end along the dimension named above; each array names one. Nothing has to cross between parts.
Inputs may be any that keep to these rules, and one draw needn't show every extreme that they name: `kept_count`: the counts of the 16 devices sum to 8192. `kept_entry`: entries may repeat. `row_owner`: among the 640 slots of one device every owner is named by exactly 40 slots.
All inputs are finite; a program needn't handle non-finite values.
Results may differ from a plain program's by a relative error of at most 0.0004.
Values may be sent and summed in bfloat16 or wider, within the bound.
A program may use at most 64 MiB of HBM per device.

v0:
```python
import functools

import jax
import jax.numpy as jnp
from jax import lax
from jax.experimental import pallas as pl
from jax.experimental.pallas import tpu as pltpu
from jax.sharding import PartitionSpec as P

KV_HEADS = 8
GROUP = 8
HEAD_DIM = 128
POOL = 7
LOG2E = 1.4426950408889634
LANES = 128
MESH = pl.DeviceIdType.MESH
NT = (((1,), (1,)), ((), ()))


def iota(shape, dim):
    return lax.broadcasted_iota(jnp.int32, shape, dim)


def kernel(
    n, cap, cap_pad, pool_scale,
    keys_hbm, vals_hbm, wq_hbm, count_ref, entry_ref, owner_ref,
    imp_ref, rows_out, score_out,
    keys, vals, qall, ebuf, stat, stat_in, stat_all, glob, rows_send, onehot, head_hot, mass, halo, ssend, srecv,
    zs, zr, ys, yr, bs, br, ts, tr, gs, gr, rs, rr, hs, hr, ss, sr, ls, es, er,
):
    G = KV_HEADS
    me = lax.axis_index("seq")
    A = n // 4
    a, b, c = me // 4, (me // 2) % 2, me % 2
    slots = entry_ref.shape[0]
    positions = keys.shape[0]
    out_slots = n * cap_pad
    qrows = qall.shape[4]
    scale = HEAD_DIM ** (-0.5)
    per_owner = n // G

    def stat_owner(g):
        return (g * per_owner + n // 2) % n

    def to(index):
        return {"seq": index}

    def remote(src, dst, ssem, rsem, index):
        return pltpu.make_async_remote_copy(
            src_ref=src, dst_ref=dst, send_sem=ssem, recv_sem=rsem,
            device_id=to(index), device_id_type=MESH,
        )

    def drain(region, sem):
        pltpu.make_async_copy(region, region, sem).wait()

    key_copy = pltpu.make_async_copy(keys_hbm, keys, ls.at[0])
    val_copy = pltpu.make_async_copy(vals_hbm, vals, ls.at[1])
    own_q = pltpu.make_async_copy(wq_hbm, qall.at[:, c, b, a], ls.at[2])
    own_q.start()
    key_copy.start()
    val_copy.start()
    barrier = pltpu.get_barrier_semaphore()

    @pl.loop(1, n)
    def _(k):
        pl.semaphore_signal(barrier, inc=1, device_id=to(lax.rem(me + k, n)), device_id_type=MESH)

    entry = entry_ref[...].reshape(1, slots)
    owner = owner_ref[...].reshape(1, slots)
    live = iota((1, slots), 1) < count_ref[0]
    owner_live = jnp.where(live, owner, -1)
    member = jnp.where(iota((n, slots), 0) == owner_live, 1.0, 0.0)
    before = jnp.where(iota((slots, slots), 0) < iota((slots, slots), 1), 1.0, 0.0).astype(jnp.bfloat16)
    earlier = jnp.dot(member.astype(jnp.bfloat16), before, preferred_element_type=jnp.float32)
    rank = jnp.sum(member * earlier, axis=0, keepdims=True)
    target = jnp.where(live, owner * cap_pad + rank.astype(jnp.int32), -1)
    head = jnp.zeros((1, slots), jnp.int32)
    for h in range(1, G):
        head = head + jnp.where(entry >= h * positions, 1, 0)
    token = entry - head * positions
    token_f = (token + 1).astype(jnp.float32)
    head_f = head.astype(jnp.float32)
    head_sel = jnp.where(iota((G, slots), 0) == head, 1.0, 0.0).astype(jnp.bfloat16)
    blk = 256
    for i in range(out_slots // blk):
        hit = (iota((blk, slots), 0) + i * blk) == target
        tok = jnp.sum(jnp.where(hit, token_f, 0.0), axis=1, keepdims=True).astype(jnp.int32) - 1
        onehot[i * blk:(i + 1) * blk, :] = jnp.where(
            iota((blk, positions), 1) == tok, 1.0, 0.0
        ).astype(jnp.bfloat16)
        hit_b = jnp.where(hit, 1.0, 0.0).astype(jnp.bfloat16)
        head_hot[:, i * blk:(i + 1) * blk] = lax.dot_general(
            head_sel, hit_b, NT, preferred_element_type=jnp.float32
        )

    own_q.wait()
    pl.semaphore_wait(barrier, n - 1)

    @pl.loop(0, G)
    def _(g):
        @pl.loop(1, A)
        def _(k):
            peer = lax.rem(a + k, A) * 4 + b * 2 + c
            remote(qall.at[g, c, b, a], qall.at[g, c, b, a], zs.at[g], zr.at[g], peer).start()

    key_copy.wait()
    val_copy.wait()

    for i in range(out_slots // blk):
        hit = (iota((blk, slots), 0) + i * blk) == target
        hcol = jnp.sum(jnp.where(hit, head_f, 0.0), axis=1, keepdims=True).astype(jnp.int32)
        hcol = jnp.broadcast_to(hcol, (blk, HEAD_DIM))
        pick = onehot[i * blk:(i + 1) * blk, :]
        for side, source in enumerate((keys, vals)):
            got = jnp.dot(pick, source[...], preferred_element_type=jnp.float32)
            chosen = jnp.zeros((blk, HEAD_DIM), jnp.float32)
            for h in range(G):
                chosen = jnp.where(hcol == h, got[:, h * HEAD_DIM:(h + 1) * HEAD_DIM], chosen)
            rows_send[
                i * blk:(i + 1) * blk,
                side * HEAD_DIM:(side + 1) * HEAD_DIM,
            ] = chosen.astype(jnp.bfloat16)

    def join(g, gathered):
        gathered[me] = stat[g]
        top = gathered[0, 0]
        for d in range(1, n):
            top = jnp.maximum(top, gathered[d, 0])
        total = jnp.zeros_like(top)
        for d in range(n):
            total = total + gathered[d, 1] * jnp.exp(gathered[d, 0] - top)
        glob[g, 0] = top
        glob[g, 1] = 1.0 / total

    def combine(g):
        @pl.when(me == stat_owner(g))
        def _():
            drain(stat_in.at[pl.ds(0, n - 1)], tr.at[0])
            join(g, stat_in)

            @pl.loop(1, n)
            def _(k):
                remote(glob.at[g], glob.at[g], gs.at[0], gr.at[g], lax.rem(me + k, n)).start()

    chunk = 2 * LANES
    tblk = 256

    def compute(g):
        group_q = qall.at[g].reshape(qall.shape[1] * qall.shape[2] * A * qrows, HEAD_DIM)
        total_rows = group_q.shape[0]
        key_cols = pl.ds(pl.multiple_of(g * HEAD_DIM, HEAD_DIM), HEAD_DIM)

        @pl.loop(0, total_rows // chunk)
        def _(j):
            qs = group_q[pl.ds(pl.multiple_of(j * chunk, chunk), chunk), :]
            lanes = pl.ds(pl.multiple_of(j * chunk, chunk), chunk)
            top8 = None
            for t in range(positions // tblk):
                s = lax.dot_general(
                    keys[t * tblk:(t + 1) * tblk, key_cols], qs, NT, preferred_element_type=jnp.float32
                )
                ebuf[g, t * tblk:(t + 1) * tblk, lanes] = s
                part = jnp.max(s.reshape(tblk // 8, 8, chunk), axis=0)
                top8 = part if top8 is None else jnp.maximum(top8, part)
            top = jnp.max(top8, axis=0, keepdims=True)
            sum8 = jnp.zeros((8, chunk), jnp.float32)
            for t in range(positions // tblk):
                s = ebuf[g, t * tblk:(t + 1) * tblk, lanes]
                e = jnp.exp2((s - top) * (scale * LOG2E))
                ebuf[g, t * tblk:(t + 1) * tblk, lanes] = e
                sum8 = sum8 + jnp.sum(e.reshape(tblk // 8, 8, chunk), axis=0)
            total = jnp.sum(sum8, axis=0, keepdims=True)
            top = top * scale
            for i in range(chunk // LANES):
                stat[g, 0, pl.ds(j * (chunk // LANES) + i, 1), :] = top[:, i * LANES:(i + 1) * LANES]
                stat[g, 1, pl.ds(j * (chunk // LANES) + i, 1), :] = total[:, i * LANES:(i + 1) * LANES]

        dest = stat_owner(g)

        @pl.when((g < G - 1) & (me != dest))
        def _():
            remote(stat.at[g], stat_in.at[me], ts.at[g], tr.at[0], dest).start()

        @pl.when(g == G - 1)
        def _():
            @pl.loop(1, n)
            def _(k):
                remote(stat.at[g], stat_all.at[me], es.at[0], er.at[0], lax.rem(me + k, n)).start()

    rows3 = rows_send.reshape(n, cap_pad, 2 * HEAD_DIM)
    own_rows = pltpu.make_async_copy(rows3.at[me], rows_out.at[me], ls.at[3])
    own_rows.start()
    mid_peer = a * 4 + (1 - b) * 2 + c
    core_peer = a * 4 + b * 2 + (1 - c)

    lag = 5

    @pl.loop(0, G + 2)
    def _(step):
        @pl.when(step < G)
        def _():
            g = step
            drain(qall.at[g, c, b, pl.ds(0, A - 1)], zr.at[g])
            remote(qall.at[g, c, b], qall.at[g, c, b], ys.at[g], yr.at[g], mid_peer).start()

        @pl.when(step == G // 2)
        def _():
            @pl.loop(1, n)
            def _(k):
                peer = lax.rem(me + k, n)
                remote(rows3.at[peer], rows_out.at[me], rs.at[0], rr.at[0], peer).start()

        @pl.when((step >= 1) & (step < G + 1))
        def _():
            g = step - 1
            drain(qall.at[g, c, 1 - b], yr.at[g])
            remote(qall.at[g, c], qall.at[g, c], bs.at[g], br.at[g], core_peer).start()

        @pl.when((step >= 2) & (step < G + 2))
        def _():
            g = step - 2
            drain(qall.at[g, 1 - c], br.at[g])
            compute(g)

        @pl.when(step >= lag)
        def _():
            combine(step - lag)

    @pl.loop(G + 2 - lag, G - 1)
    def _(g):
        combine(g)

    ones = jnp.ones((8, LANES), jnp.float32)

    @pl.loop(0, G)
    def _(g):
        @pl.when((g < G - 1) & (me != stat_owner(g)))
        def _():
            drain(glob.at[g], gr.at[g])

        @pl.when(g == G - 1)
        def _():
            drain(stat_all.at[pl.ds(0, n - 1)], er.at[0])
            join(g, stat_all)

        weight = jnp.exp(stat[g, 0] - glob[g, 0]) * glob[g, 1]
        for t in range(positions // LANES):
            acc = ebuf[g, t * LANES:(t + 1) * LANES, 0:LANES] * weight[0:1, :]
            for k in range(1, weight.shape[0]):
                acc = acc + ebuf[g, t * LANES:(t + 1) * LANES, k * LANES:(k + 1) * LANES] * weight[k:k + 1, :]
            line = lax.dot_general(
                ones, acc, NT, preferred_element_type=jnp.float32, precision=lax.Precision.HIGHEST
            )
            mass[g, :, t * LANES:(t + 1) * LANES] = line[0:1, :]

    halo[0] = jnp.zeros((G, LANES), jnp.float32)
    halo[1] = jnp.zeros((G, LANES), jnp.float32)
    column = jnp.concatenate([mass[g] for g in range(G)], axis=0)
    halo[4] = column[:, 0:LANES]
    halo[5] = column[:, positions - LANES:]
    low_copy = remote(halo.at[4], halo.at[3], hs.at[0], hr.at[0], lax.rem(me + n - 1, n))
    high_copy = remote(halo.at[5], halo.at[2], hs.at[1], hr.at[1], lax.rem(me + 1, n))

    @pl.when(me > 0)
    def _():
        low_copy.start()

    @pl.when(me < n - 1)
    def _():
        high_copy.start()

    @pl.when(me > 0)
    def _():
        drain(halo.at[2], hr.at[1])
        halo[0] = halo[2]

    @pl.when(me < n - 1)
    def _():
        drain(halo.at[3], hr.at[0])
        halo[1] = halo[3]

    padded = jnp.concatenate([halo[0], column, halo[1]], axis=1)
    width = padded.shape[1]
    pooled = padded
    for o in range(1, POOL // 2 + 1):
        pooled = pooled + pltpu.roll(padded, o, 1) + pltpu.roll(padded, width - o, 1)
    importance = pooled[:, LANES:LANES + positions] * pool_scale
    imp_ref[...] = importance

    got = lax.dot_general(
        importance.astype(jnp.bfloat16), onehot[...], NT, preferred_element_type=jnp.float32
    )
    line = jnp.sum(got * head_hot[...], axis=0, keepdims=True)
    owner_of = iota((n, out_slots), 1) - iota((n, out_slots), 0) * cap_pad
    spread = jnp.where((owner_of >= 0) & (owner_of < cap_pad), line, 0.0).astype(jnp.bfloat16)
    row_id, lane_id = iota((out_slots, LANES), 0), iota((out_slots, LANES), 1)
    fold = (row_id - lane_id) % cap_pad == 0
    fold = jnp.where(fold & (lane_id < cap_pad), 1.0, 0.0).astype(jnp.bfloat16)
    table = jnp.dot(spread, fold, preferred_element_type=jnp.float32)
    for k in range(n):
        ssend[k] = table[k:k + 1, :]

    @pl.loop(1, n)
    def _(k):
        peer = lax.rem(me + k, n)
        remote(ssend.at[peer], srecv.at[me], ss.at[0], sr.at[0], peer).start()

    own_rows.wait()
    drain(rows_out.at[pl.ds(0, n - 1)], rr.at[0])
    drain(rows3.at[pl.ds(0, n - 1)], rs.at[0])

    @pl.loop(0, G)
    def _(g):
        drain(qall.at[g, c, b, pl.ds(0, A - 1)], zs.at[g])
        drain(qall.at[g, c, b], ys.at[g])
        drain(qall.at[g, c], bs.at[g])

        @pl.when((g < G - 1) & (me != stat_owner(g)))
        def _():
            drain(stat.at[g], ts.at[g])

        @pl.when((g < G - 1) & (me == stat_owner(g)))
        def _():
            drain(stat_in.at[pl.ds(0, n - 1)], gs.at[0])

    @pl.when(me > 0)
    def _():
        drain(halo.at[4], hs.at[0])

    @pl.when(me < n - 1)
    def _():
        drain(halo.at[5], hs.at[1])

    drain(stat_all.at[pl.ds(0, n - 1)], es.at[0])
    drain(ssend.at[pl.ds(0, n - 1)], ss.at[0])
    drain(srecv.at[pl.ds(0, n - 1)], sr.at[0])
    srecv[me] = ssend[me]
    score_out[...] = srecv[...]


def finish(cap, imp_in, rows_in, score_in, imp_ref, rows_ref, score_ref):
    n = rows_in.shape[0]
    imp_ref[...] = imp_in[...]
    rows_ref[...] = rows_in[:, 0:cap, :]
    table = jnp.concatenate([score_in[k] for k in range(n)], axis=0).astype(jnp.bfloat16)
    column = iota((LANES, n * cap), 1) - iota((LANES, n * cap), 0)
    unfold = jnp.where(column % cap == 0, 1.0, 0.0)
    unfold = jnp.where(iota((LANES, n * cap), 0) < cap, unfold, 0.0).astype(jnp.bfloat16)
    wide = jnp.dot(table, unfold, preferred_element_type=jnp.float32)
    within = iota((n, n * cap), 1) - iota((n, n * cap), 0) * cap
    line = jnp.sum(jnp.where((within >= 0) & (within < cap), wide, 0.0), axis=0, keepdims=True)
    score_ref[...] = line.astype(jnp.bfloat16).reshape(n * cap)


def per_device(n, cached_keys, cached_values, window_queries, kept_count, kept_entry, row_owner):
    positions, width = cached_keys.shape
    slots = kept_entry.shape[0]
    cap = slots // n
    cap_pad = -(-cap // 16) * 16
    query_rows = window_queries.shape[0]
    heads = window_queries.shape[1] // HEAD_DIM
    group = heads // KV_HEADS
    window = query_rows * n
    qrows = query_rows * group
    lane_rows = n * qrows // LANES
    wq = (
        window_queries.reshape(query_rows, heads, HEAD_DIM)
        .transpose(1, 0, 2)
        .reshape(KV_HEADS, qrows, HEAD_DIM)
    )
    pool_scale = n * positions / (group * window * POOL)
    any_spec = pl.BlockSpec(memory_space=pl.ANY)
    vmem = pl.BlockSpec(memory_space=pltpu.VMEM)
    dma = pltpu.SemaphoreType.DMA
    A = n // 4
    f32, bf16 = jnp.float32, jnp.bfloat16
    importance, rows, score = pl.pallas_call(
        functools.partial(kernel, n, cap, cap_pad, pool_scale),
        out_shape=(
            jax.ShapeDtypeStruct((KV_HEADS, positions), f32),
            jax.ShapeDtypeStruct((n, cap_pad, 2 * HEAD_DIM), bf16),
            jax.ShapeDtypeStruct((n, 1, LANES), f32),
        ),
        in_specs=[any_spec, any_spec, any_spec, pl.BlockSpec(memory_space=pltpu.SMEM), vmem, vmem],
        out_specs=(vmem, any_spec, vmem),
        scratch_shapes=[
            pltpu.VMEM((positions, width), bf16),
            pltpu.VMEM((positions, width), bf16),
            pltpu.VMEM((KV_HEADS, 2, 2, A, qrows, HEAD_DIM), bf16),
            pltpu.VMEM((KV_HEADS, positions, n * qrows), f32),
            pltpu.VMEM((KV_HEADS, 2, lane_rows, LANES), f32),
            pltpu.VMEM((n, 2, lane_rows, LANES), f32),
            pltpu.VMEM((n, 2, lane_rows, LANES), f32),
            pltpu.VMEM((KV_HEADS, 2, lane_rows, LANES), f32),
            pltpu.VMEM((n * cap_pad, 2 * HEAD_DIM), bf16),
            pltpu.VMEM((n * cap_pad, positions), bf16),
            pltpu.VMEM((KV_HEADS, n * cap_pad), f32),
            pltpu.VMEM((KV_HEADS, 1, positions), f32),
            pltpu.VMEM((6, KV_HEADS, LANES), f32),
            pltpu.VMEM((n, 1, LANES), f32),
            pltpu.VMEM((n, 1, LANES), f32),
        ]
        + [dma((KV_HEADS,))] * 6
        + [dma((KV_HEADS,)), dma((1,)), dma((1,)), dma((KV_HEADS,)), dma((1,)), dma((1,))]
        + [dma((2,)), dma((2,)), dma((1,)), dma((1,)), dma((4,)), dma((1,)), dma((1,))],
        compiler_params=pltpu.CompilerParams(
            collective_id=0, has_side_effects=True, vmem_limit_bytes=60 * 1024 * 1024
        ),
        name="snap",
    )(cached_keys, cached_values, wq, kept_count, kept_entry, row_owner)
    importance, rows, score = pl.pallas_call(
        functools.partial(finish, cap),
        out_shape=(
            jax.ShapeDtypeStruct((KV_HEADS, positions), f32),
            jax.ShapeDtypeStruct((n, cap, 2 * HEAD_DIM), bf16),
            jax.ShapeDtypeStruct((n * cap,), bf16),
        ),
        in_specs=[vmem, vmem, vmem],
        out_specs=(vmem, vmem, vmem),
        name="finish",
    )(importance, rows, score)
    return importance, rows.reshape(n * cap, 2 * HEAD_DIM), score


def solution(mesh):
    n = mesh.shape["seq"]
    split = P(("rep", "seq"))
    wide = P(("rep", "seq"), None)
    return jax.shard_map(
        functools.partial(per_device, n),
        mesh=mesh,
        in_specs=(wide, wide, wide, split, split, split),
        out_specs=(P("rep", "seq"), wide, split),
        check_vma=False,
    )
```

profile of v0, /device:TPU:0, one launch (start us, length us, event | category | flops | bytes accessed | tf_op | source)
XLA Modules:
  0.0 58.4 jit_solution(11042464434979427484)
XLA Ops:
  1.3 55.3 %snap.1 = (f32[8,1024]{1,0:T(8,128)}, bf16[16,48,256]{2,1,0:T(8,128)(2,1)}, f32[16,1,128]{2,1,0:T(1,128)}) custom-call(bf16[1024,1024]{1,0:T(8,128)(2,1)} %keys_hbm.1, bf16[1024,1024]{1,0:T(8,128)(2,1)} %vals_hbm.1, bf16[8,64,128]{2,1,0:T(8,128)(2,1)} %bitcast.6, s32[1]{0:T(128)S(6)} %copy.9.count_ref, s32[640]{0:T(1024)} %entry_ref.1, s32[640]{0:T(1024)} %owner_ref.1), custom_call_target="tpu_custom_call" | custom-call | tf_op jit(solution)/shard_map/snap/pallas_call | solution.py:378
  56.6 1.8 %finish.1 = (f32[8,1024]{1,0:T(8,128)}, bf16[16,40,256]{2,1,0:T(8,128)(2,1)}, bf16[640]{0:T(1024)(128)(2,1)}) custom-call(f32[8,1024]{1,0:T(8,128)} %get-tuple-element.9.imp_in, bf16[16,48,256]{2,1,0:T(8,128)(2,1)} %get-tuple-element.10.rows_in, f32[16,1,128]{2,1,0:T(1,128)} %get-tuple-element.11.score_in), custom_call_target="tpu_custom_call" | custom-call | tf_op jit(solution)/shard_map/finish/pallas_call | solution.py:412
where the time goes:
time: 58.6 us; the launch traced here: 58.4 us
  Pallas kernels  57.1 us (97%)
  between operations  1.29 us (2%)
    pallas_call x1, Pallas kernels, per_device(): pl.pallas_call(functools.partial(kernel, n, cap, cap_pad, pool_scale), ou...  55.3 us
    pallas_call x1, Pallas kernels, per_device(): pl.pallas_call(functools.partial(finish, cap), out_shape=(jax.ShapeDtypeS...  1.79 us

commit v1 on v0

v1 whole, which is shorter than its diff:
```python
import functools

import jax
import jax.numpy as jnp
from jax import lax
from jax.experimental import pallas as pl
from jax.experimental.pallas import tpu as pltpu
from jax.sharding import PartitionSpec as P

KV_HEADS = 8
GROUP = 8
HEAD_DIM = 128
POOL = 7
LOG2E = 1.4426950408889634
LANES = 128
EDGE = 16
STRIP = 64
MESH = pl.DeviceIdType.MESH
NT = (((1,), (1,)), ((), ()))


def iota(shape, dim):
    return lax.broadcasted_iota(jnp.int32, shape, dim)


def kernel(
    n, cap, cap_pad, pool_scale,
    keys_hbm, vals_hbm, wq_hbm, count_hbm, entry_hbm, owner_hbm,
    imp_ref, rows_out, score_out,
    keys, vals, qall, ebuf, raw, peak, sums, stat, stat_in, stat_all, glob, rows_send, onehot, slot_tile, slot_lane,
    mass, edge, ssend, srecv, count_ref, entry_ref, owner_ref,
    zs, zr, ws, wr, ys, yr, bs, br, ts, tr, gs, gr, rs, rr, hs, hr, ss, sr, ls, es, er,
):
    G = KV_HEADS
    me = lax.axis_index("seq")
    A = n // 4
    A1 = A // 2
    a, b, c = me // 4, (me // 2) % 2, me % 2
    a1, a0 = a // 2, a % 2
    slots = entry_ref.shape[0]
    positions = vals.shape[0]
    tiles = positions // LANES
    out_slots = n * cap_pad
    queries = ebuf.shape[2]
    scale2 = HEAD_DIM ** (-0.5) * LOG2E
    per_owner = n // G

    def stat_owner(g):
        return (g * per_owner + n // 2) % n

    def to(index):
        return {"seq": index}

    def remote(src, dst, ssem, rsem, index):
        return pltpu.make_async_remote_copy(
            src_ref=src, dst_ref=dst, send_sem=ssem, recv_sem=rsem,
            device_id=to(index), device_id_type=MESH,
        )

    def drain(region, sem):
        pltpu.make_async_copy(region, region, sem).wait()

    barrier = pltpu.get_barrier_semaphore()

    @pl.loop(1, n)
    def _(k):
        pl.semaphore_signal(barrier, inc=1, device_id=to(lax.rem(me + k, n)), device_id_type=MESH)

    own_q = pltpu.make_async_copy(wq_hbm, qall.at[:, c, b, a0, a1], ls.at[2])
    small = [
        pltpu.make_async_copy(src, dst, ls.at[4 + i])
        for i, (src, dst) in enumerate(((count_hbm, count_ref), (entry_hbm, entry_ref), (owner_hbm, owner_ref)))
    ]
    key_copy = pltpu.make_async_copy(keys_hbm, keys.at[pl.ds(0, positions)], ls.at[0])
    val_copy = pltpu.make_async_copy(vals_hbm, vals, ls.at[1])
    own_q.start()
    for copy in small:
        copy.start()
    key_copy.start()
    val_copy.start()

    low, high = lax.rem(me + n - 1, n), lax.rem(me + 1, n)
    mid_peer = a * 4 + (1 - b) * 2 + c
    core_peer = a * 4 + b * 2 + (1 - c)
    step_peer = (a + 1 - 2 * a0) * 4 + b * 2 + c
    first_rows = pl.ds(0, EDGE)
    last_rows = pl.ds(positions - EDGE, EDGE)
    from_low = pl.ds(positions, EDGE)
    from_high = pl.ds(positions + EDGE, EDGE)

    @pl.when(me == 0)
    def _():
        keys[positions:positions + EDGE, :] = jnp.zeros((EDGE, keys.shape[1]), keys.dtype)

    @pl.when(me == n - 1)
    def _():
        keys[positions + EDGE:positions + 2 * EDGE, :] = jnp.zeros((EDGE, keys.shape[1]), keys.dtype)

    def greet():
        own_q.wait()
        pl.semaphore_wait(barrier, n - 1)

        @pl.loop(0, G)
        def _(g):
            mine = qall.at[g, c, b, a0, a1]

            @pl.loop(1, A1)
            def _(k):
                peer = (lax.rem(a1 + k, A1) * 2 + a0) * 4 + b * 2 + c
                remote(mine, mine, zs.at[g], zr.at[g], peer).start()

            remote(mine, mine, ys.at[g], yr.at[g], mid_peer).start()

        @pl.when(me > 0)
        def _():
            remote(keys_hbm.at[first_rows], keys.at[from_high], hs.at[0], hr.at[0], low).start()

        @pl.when(me < n - 1)
        def _():
            remote(keys_hbm.at[last_rows], keys.at[from_low], hs.at[1], hr.at[1], high).start()

    late = me >= n // 2

    @pl.when(late)
    def _():
        greet()

    for copy in small:
        copy.wait()
    entry = entry_ref[...].reshape(1, slots)
    owner = owner_ref[...].reshape(1, slots)
    live = iota((1, slots), 1) < count_ref[0]
    owner_live = jnp.where(live, owner, -1)
    member = jnp.where(iota((n, slots), 0) == owner_live, 1.0, 0.0)
    before = jnp.where(iota((slots, slots), 0) < iota((slots, slots), 1), 1.0, 0.0).astype(jnp.bfloat16)
    earlier = jnp.dot(member.astype(jnp.bfloat16), before, preferred_element_type=jnp.float32)
    rank = jnp.sum(member * earlier, axis=0, keepdims=True).astype(jnp.int32)
    target = jnp.where(live, owner * cap_pad + rank, -1)
    tile_of = entry // LANES
    lane_of = entry - tile_of * LANES
    head = tile_of // tiles
    token_f = (entry - head * positions + 1).astype(jnp.float32)
    head_f = head.astype(jnp.float32)
    at_rank = jnp.where(iota((LANES, slots), 0) == rank, 1.0, 0.0).astype(jnp.bfloat16)

    def by_rank(value):
        marked = (member * value.astype(jnp.float32)).astype(jnp.bfloat16)
        return lax.dot_general(marked, at_rank, NT, preferred_element_type=jnp.float32).astype(jnp.int32)

    slot_tile[...] = by_rank(tile_of + 1)
    slot_lane[...] = by_rank(lane_of)

    @pl.when(jnp.logical_not(late))
    def _():
        greet()

    key_copy.wait()
    val_copy.wait()

    def gather_rows(k0, count):
        blk = count * cap_pad
        hit = (iota((blk, slots), 0) + k0 * cap_pad) == target
        tok = jnp.sum(jnp.where(hit, token_f, 0.0), axis=1, keepdims=True).astype(jnp.int32) - 1
        hcol = jnp.sum(jnp.where(hit, head_f, 0.0), axis=1, keepdims=True).astype(jnp.int32)
        hcol = jnp.broadcast_to(hcol, (blk, HEAD_DIM))
        onehot[...] = jnp.where(iota((blk, positions), 1) == tok, 1.0, 0.0).astype(jnp.bfloat16)
        for side, source in enumerate((keys, vals)):
            got = jnp.dot(onehot[...], source[0:positions, :], preferred_element_type=jnp.float32)
            chosen = jnp.zeros((blk, HEAD_DIM), jnp.float32)
            for h in range(G):
                chosen = jnp.where(hcol == h, got[:, h * HEAD_DIM:(h + 1) * HEAD_DIM], chosen)
            for k in range(count):
                rows_send[k0 + k, :, side * HEAD_DIM:(side + 1) * HEAD_DIM] = chosen[
                    k * cap_pad:(k + 1) * cap_pad
                ].astype(jnp.bfloat16)

    per = onehot.shape[0] // cap_pad
    for i in range(n // per):
        gather_rows(i * per, per)

    def lse(values):
        top = values[0]
        for x in values[1:]:
            top = jnp.maximum(top, x)
        total = jnp.zeros_like(top)
        for x in values:
            total = total + jnp.exp2(x - top)
        return top + jnp.log(total) * LOG2E

    def join(g, gathered):
        gathered[me] = stat[g]
        glob[g] = lse([gathered[d] for d in range(n)])

    def combine(g):
        @pl.when(me == stat_owner(g))
        def _():
            drain(stat_in.at[pl.ds(0, n - 1)], tr.at[0])
            join(g, stat_in)

            @pl.loop(1, n)
            def _(k):
                remote(glob.at[g], glob.at[g], gs.at[0], gr.at[g], lax.rem(me + k, n)).start()

    chunk = 2 * LANES
    strip = sums.shape[0]
    span = positions // strip

    def compute(g):
        group_q = qall.at[g].reshape(queries, HEAD_DIM)
        key_cols = pl.ds(pl.multiple_of(g * HEAD_DIM, HEAD_DIM), HEAD_DIM)
        for j in range(queries // chunk):
            lanes = slice(j * chunk, (j + 1) * chunk)
            s = lax.dot_general(
                keys[:, key_cols], group_q[lanes, :], NT, preferred_element_type=jnp.float32
            )
            for u in range(strip):
                x = s[u * span:(u + 1) * span].reshape(span // 8, 8, chunk)
                top = jnp.max(x, axis=0)
                e = jnp.exp2((x - top[None]) * scale2)
                ebuf[g, u * span:(u + 1) * span, lanes] = e.reshape(span, chunk)
                peak[g, u, :, lanes] = top
                sums[u, :, lanes] = jnp.sum(e, axis=0)
            raw[g, 0:8, lanes] = s[positions + EDGE - 8:positions + EDGE]
            raw[g, 8:16, lanes] = s[positions + EDGE:positions + EDGE + 8]
        tops = peak[g]
        top = jnp.max(jnp.max(tops, axis=0), axis=0, keepdims=True)
        total = jnp.sum(jnp.sum(sums[...] * jnp.exp2((tops - top[None]) * scale2), axis=0), axis=0, keepdims=True)
        local = top * scale2 + jnp.log(total) * LOG2E
        for i in range(queries // LANES):
            stat[g, i:i + 1, :] = local[:, i * LANES:(i + 1) * LANES]

        dest = stat_owner(g)

        @pl.when((g < G - 1) & (me != dest))
        def _():
            remote(stat.at[g], stat_in.at[me], ts.at[g], tr.at[0], dest).start()

        @pl.when(g == G - 1)
        def _():
            @pl.loop(1, n)
            def _(k):
                remote(stat.at[g], stat_all.at[me], es.at[0], er.at[0], lax.rem(me + k, n)).start()

    own_rows = pltpu.make_async_copy(rows_send.at[me], rows_out.at[me], ls.at[3])
    own_rows.start()

    lag = 8

    @pl.loop(0, G + 5)
    def _(step):
        @pl.when(step < G)
        def _():
            g = step
            drain(qall.at[g, c, b, a0, pl.ds(0, A1 - 1)], zr.at[g])
            mine = qall.at[g, c, b, a0]
            remote(mine, mine, ws.at[g], wr.at[g], step_peer).start()

            @pl.loop(1, A1)
            def _(k):
                other = qall.at[g, c, b, a0, lax.rem(a1 + k, A1)]
                remote(other, other, ys.at[g], yr.at[g], mid_peer).start()

        @pl.when((step >= 2) & (step < G + 2))
        def _():
            g = step - 2
            drain(qall.at[g, c, b, 1 - a0], wr.at[g])
            other = qall.at[g, c, b, 1 - a0]
            remote(other, other, ys.at[g], yr.at[g], mid_peer).start()

        @pl.when((step >= 4) & (step < G + 4))
        def _():
            g = step - 4
            drain(qall.at[g, c, 1 - b], yr.at[g])
            remote(qall.at[g, c], qall.at[g, c], bs.at[g], br.at[g], core_peer).start()

        @pl.when(step == G + 1)
        def _():
            @pl.loop(1, n)
            def _(k):
                peer = lax.rem(me + k, n)
                remote(rows_send.at[peer], rows_out.at[me], rs.at[0], rr.at[0], peer).start()

        @pl.when((step == 5) & (me < n - 1))
        def _():
            drain(keys.at[from_high], hr.at[0])

        @pl.when((step == 5) & (me > 0))
        def _():
            drain(keys.at[from_low], hr.at[1])

        @pl.when(step >= 5)
        def _():
            g = step - 5
            drain(qall.at[g, 1 - c], br.at[g])
            compute(g)

        @pl.when(step >= lag)
        def _():
            combine(step - lag)

    @pl.loop(G + 5 - lag, G - 1)
    def _(g):
        combine(g)

    @pl.loop(0, G)
    def _(g):
        @pl.when((g < G - 1) & (me != stat_owner(g)))
        def _():
            drain(glob.at[g], gr.at[g])

        @pl.when(g == G - 1)
        def _():
            drain(stat_all.at[pl.ds(0, n - 1)], er.at[0])
            join(g, stat_all)

        whole = glob[g]
        level = [whole[k:k + 1, :] for k in range(queries // LANES)]

        def weighted(value, k):
            return value * weight[:, k * LANES:(k + 1) * LANES][None]

        for t in range(tiles):
            acc = None
            for u in range(t * LANES // span, max((t + 1) * LANES // span, t * LANES // span + 1)):
                weight = jnp.concatenate(
                    [
                        jnp.exp2(peak[g, u, :, k * LANES:(k + 1) * LANES] * scale2 - level[k])
                        for k in range(queries // LANES)
                    ],
                    axis=1,
                )
                r0 = max(u * span, t * LANES)
                rows = min(span, LANES)
                part = None
                for k in range(queries // LANES):
                    e = ebuf[g, r0:r0 + rows, k * LANES:(k + 1) * LANES].reshape(rows // 8, 8, LANES)
                    e = weighted(e, k)
                    part = e if part is None else part + e
                part = part.reshape(rows, LANES)
                acc = part if acc is None else jnp.concatenate([acc, part], axis=0)
            mass[g, :, t * LANES:(t + 1) * LANES] = jnp.sum(acc.T, axis=0, keepdims=True)
        acc = None
        for k in range(queries // LANES):
            e = jnp.exp2(raw[g, :, k * LANES:(k + 1) * LANES] * scale2 - level[k])
            acc = e if acc is None else acc + e
        edge[pl.ds(pl.multiple_of(g * 16, 16), 16), :] = acc

    column = jnp.concatenate([mass[g] for g in range(G)], axis=0)
    line = jnp.sum(edge[...].T, axis=0, keepdims=True)
    row_of = iota((G, LANES), 0)
    ends = jnp.zeros((G, LANES), jnp.float32)
    for g in range(G):
        turned = pltpu.roll(line, (LANES - 8 - 16 * g) % LANES, 1)
        ends = jnp.where(row_of == g, turned, ends)
    before_low = jnp.where(me > 0, ends, 0.0)
    after_high = jnp.where(me < n - 1, ends, 0.0)
    padded = jnp.concatenate([before_low, column, after_high], axis=1)
    width = padded.shape[1]
    pooled = padded
    for o in range(1, POOL // 2 + 1):
        pooled = pooled + pltpu.roll(padded, o, 1) + pltpu.roll(padded, width - o, 1)
    importance = pooled[:, LANES:LANES + positions] * pool_scale
    imp_ref[...] = importance

    want, lane = slot_tile[...], slot_lane[...]
    table = jnp.zeros((n, LANES), jnp.float32)
    for h in range(G):
        for t in range(tiles):
            part = jnp.broadcast_to(importance[h:h + 1, t * LANES:(t + 1) * LANES], (n, LANES))
            found = jnp.take_along_axis(part, lane, axis=1)
            table = jnp.where(want == h * tiles + t + 1, found, table)
    for k in range(n):
        ssend[k] = table[k:k + 1, :]

    @pl.loop(1, n)
    def _(k):
        peer = lax.rem(me + k, n)
        remote(ssend.at[peer], srecv.at[me], ss.at[0], sr.at[0], peer).start()

    own_rows.wait()
    drain(rows_out.at[pl.ds(0, n - 1)], rr.at[0])
    drain(rows_send.at[pl.ds(0, n - 1)], rs.at[0])

    @pl.loop(0, G)
    def _(g):
        drain(qall.at[g, c, b, a0, pl.ds(0, A1 - 1)], zs.at[g])
        drain(qall.at[g, c, b, a0], ws.at[g])
        drain(qall.at[g, c, b], ys.at[g])
        drain(qall.at[g, c], bs.at[g])

        @pl.when((g < G - 1) & (me != stat_owner(g)))
        def _():
            drain(stat.at[g], ts.at[g])

        @pl.when((g < G - 1) & (me == stat_owner(g)))
        def _():
            drain(stat_in.at[pl.ds(0, n - 1)], gs.at[0])

    @pl.when(me > 0)
    def _():
        drain(keys.at[from_high], hs.at[0])

    @pl.when(me < n - 1)
    def _():
        drain(keys.at[from_low], hs.at[1])

    drain(stat_all.at[pl.ds(0, n - 1)], es.at[0])
    drain(ssend.at[pl.ds(0, n - 1)], ss.at[0])
    drain(srecv.at[pl.ds(0, n - 1)], sr.at[0])
    srecv[me] = ssend[me]
    score_out[...] = srecv[...]


def finish(cap, imp_in, rows_in, score_in, imp_ref, rows_ref, score_ref):
    n = rows_in.shape[0]
    imp_ref[...] = imp_in[...]
    rows_ref[...] = rows_in[:, 0:cap, :]
    table = jnp.concatenate([score_in[k] for k in range(n)], axis=0).astype(jnp.bfloat16)
    column = iota((LANES, n * cap), 1) - iota((LANES, n * cap), 0)
    unfold = jnp.where(column % cap == 0, 1.0, 0.0)
    unfold = jnp.where(iota((LANES, n * cap), 0) < cap, unfold, 0.0).astype(jnp.bfloat16)
    wide = jnp.dot(table, unfold, preferred_element_type=jnp.float32)
    within = iota((n, n * cap), 1) - iota((n, n * cap), 0) * cap
    line = jnp.sum(jnp.where((within >= 0) & (within < cap), wide, 0.0), axis=0, keepdims=True)
    score_ref[...] = line.astype(jnp.bfloat16).reshape(n * cap)


def per_device(n, cached_keys, cached_values, window_queries, kept_count, kept_entry, row_owner):
    positions, width = cached_keys.shape
    slots = kept_entry.shape[0]
    cap = slots // n
    cap_pad = -(-cap // 8) * 8
    query_rows = window_queries.shape[0]
    heads = window_queries.shape[1] // HEAD_DIM
    group = heads // KV_HEADS
    window = query_rows * n
    qrows = query_rows * group
    lane_rows = n * qrows // LANES
    wq = (
        window_queries.reshape(query_rows, heads, HEAD_DIM)
        .transpose(1, 0, 2)
        .reshape(KV_HEADS, qrows, HEAD_DIM)
    )
    pool_scale = n * positions / (group * window * POOL)
    any_spec = pl.BlockSpec(memory_space=pl.ANY)
    vmem = pl.BlockSpec(memory_space=pltpu.VMEM)
    dma = pltpu.SemaphoreType.DMA
    A = n // 4
    f32, bf16 = jnp.float32, jnp.bfloat16
    importance, rows, score = pl.pallas_call(
        functools.partial(kernel, n, cap, cap_pad, pool_scale),
        out_shape=(
            jax.ShapeDtypeStruct((KV_HEADS, positions), f32),
            jax.ShapeDtypeStruct((n, cap_pad, 2 * HEAD_DIM), bf16),
            jax.ShapeDtypeStruct((n, 1, LANES), f32),
        ),
        in_specs=[any_spec] * 6,
        out_specs=(vmem, any_spec, vmem),
        scratch_shapes=[
            pltpu.VMEM((positions + 2 * EDGE, width), bf16),
            pltpu.VMEM((positions, width), bf16),
            pltpu.VMEM((KV_HEADS, 2, 2, 2, A // 2, qrows, HEAD_DIM), bf16),
            pltpu.VMEM((KV_HEADS, positions, n * qrows), f32),
            pltpu.VMEM((KV_HEADS, 16, n * qrows), f32),
            pltpu.VMEM((KV_HEADS, positions // STRIP, 8, n * qrows), f32),
            pltpu.VMEM((positions // STRIP, 8, n * qrows), f32),
            pltpu.VMEM((KV_HEADS, lane_rows, LANES), f32),
            pltpu.VMEM((n, lane_rows, LANES), f32),
            pltpu.VMEM((n, lane_rows, LANES), f32),
            pltpu.VMEM((KV_HEADS, lane_rows, LANES), f32),
            pltpu.VMEM((n, cap_pad, 2 * HEAD_DIM), bf16),
            pltpu.VMEM((n * cap_pad // 2, positions), bf16),
            pltpu.VMEM((n, LANES), jnp.int32),
            pltpu.VMEM((n, LANES), jnp.int32),
            pltpu.VMEM((KV_HEADS, 1, positions), f32),
            pltpu.VMEM((16 * KV_HEADS, LANES), f32),
            pltpu.VMEM((n, 1, LANES), f32),
            pltpu.VMEM((n, 1, LANES), f32),
            pltpu.SMEM((1,), jnp.int32),
            pltpu.VMEM((slots,), jnp.int32),
            pltpu.VMEM((slots,), jnp.int32),
        ]
        + [dma((KV_HEADS,))] * 8
        + [dma((KV_HEADS,)), dma((1,)), dma((1,)), dma((KV_HEADS,)), dma((1,)), dma((1,))]
        + [dma((2,)), dma((2,)), dma((1,)), dma((1,)), dma((7,)), dma((1,)), dma((1,))],
        compiler_params=pltpu.CompilerParams(
            collective_id=0, has_side_effects=True, vmem_limit_bytes=60 * 1024 * 1024
        ),
        name="snap",
    )(cached_keys, cached_values, wq, kept_count, kept_entry, row_owner)
    importance, rows, score = pl.pallas_call(
        functools.partial(finish, cap),
        out_shape=(
            jax.ShapeDtypeStruct((KV_HEADS, positions), f32),
            jax.ShapeDtypeStruct((n, cap, 2 * HEAD_DIM), bf16),
            jax.ShapeDtypeStruct((n * cap,), bf16),
        ),
        in_specs=[vmem, vmem, vmem],
        out_specs=(vmem, vmem, vmem),
        name="finish",
    )(importance, rows, score)
    return importance, rows.reshape(n * cap, 2 * HEAD_DIM), score


def solution(mesh):
    n = mesh.shape["seq"]
    split = P(("rep", "seq"))
    wide = P(("rep", "seq"), None)
    return jax.shard_map(
        functools.partial(per_device, n),
        mesh=mesh,
        in_specs=(wide, wide, wide, split, split, split),
        out_specs=(P("rep", "seq"), wide, split),
        check_vma=False,
    )
```

time: 58.6 us -> 51 us (0.87)
  Pallas kernels: 57.1 us -> 49.5 us
    pallas_call x1, Pallas kernels: 55.3 us -> 47.8 us  [per_device(): pl.pallas_call(functools.partial(kernel, n, cap, cap_pad, pool_scale), ou...]
where the time goes in v1:
time: 51 us; the launch traced here: 50.8 us
  Pallas kernels  49.5 us (97%)
  between operations  1.29 us (3%)
    pallas_call x1, Pallas kernels, per_device(): pl.pallas_call(functools.partial(kernel, n, cap, cap_pad, pool_scale), ou...  47.8 us
    pallas_call x1, Pallas kernels, per_device(): pl.pallas_call(functools.partial(finish, cap), out_shape=(jax.ShapeDtypeS...  1.76 us

profile of v1, /device:TPU:0, one launch (start us, length us, event | category | flops | bytes accessed | tf_op | source)
XLA Modules:
  0.0 50.8 jit_solution(8257533624104447672)
XLA Ops:
  1.3 47.8 %snap.1 = (f32[8,1024]{1,0:T(8,128)}, bf16[16,40,256]{2,1,0:T(8,128)(2,1)}, f32[16,1,128]{2,1,0:T(1,128)}) custom-call(bf16[1024,1024]{1,0:T(8,128)(2,1)} %keys_hbm.1, bf16[1024,1024]{1,0:T(8,128)(2,1)} %vals_hbm.1, bf16[8,64,128]{2,1,0:T(8,128)(2,1)} %bitcast.6, s32[1]{0:T(128)S(6)} %copy.9.count_hbm, s32[640]{0:T(1024)} %entry_hbm.1, s32[640]{0:T(1024)} %owner_hbm.1), custom_call_target="tpu_custom_call" | custom-call | tf_op jit(solution)/shard_map/snap/pallas_call | solution.py:450
  49.1 1.8 %finish.1 = (f32[8,1024]{1,0:T(8,128)}, bf16[16,40,256]{2,1,0:T(8,128)(2,1)}, bf16[640]{0:T(1024)(128)(2,1)}) custom-call(f32[8,1024]{1,0:T(8,128)} %get-tuple-element.9.imp_in, bf16[16,40,256]{2,1,0:T(8,128)(2,1)} %get-tuple-element.10.rows_in, f32[16,1,128]{2,1,0:T(1,128)} %get-tuple-element.11.score_in), custom_call_target="tpu_custom_call" | custom-call | tf_op jit(solution)/shard_map/finish/pallas_call | solution.py:491

commit v2 on v1

--- a/solution.py
+++ b/solution.py
@@ -26,9 +26,9 @@
 def kernel(
     n, cap, cap_pad, pool_scale,
     keys_hbm, vals_hbm, wq_hbm, count_hbm, entry_hbm, owner_hbm,
-    imp_ref, rows_out, score_out,
+    imp_out, rows_out, score_out,
     keys, vals, qall, ebuf, raw, peak, sums, stat, stat_in, stat_all, glob, rows_send, onehot, slot_tile, slot_lane,
-    mass, edge, ssend, srecv, count_ref, entry_ref, owner_ref,
+    mass, edge, ssend, imp_ref, count_ref, entry_ref, owner_ref,
     zs, zr, ws, wr, ys, yr, bs, br, ts, tr, gs, gr, rs, rr, hs, hr, ss, sr, ls, es, er,
 ):
     G = KV_HEADS
@@ -96,20 +96,24 @@
     def _():
         keys[positions + EDGE:positions + 2 * EDGE, :] = jnp.zeros((EDGE, keys.shape[1]), keys.dtype)
 
+    def send_own(g):
+        mine, place = wq_hbm.at[g], qall.at[g, c, b, a0, a1]
+
+        @pl.loop(1, A1)
+        def _(k):
+            peer = (lax.rem(a1 + k, A1) * 2 + a0) * 4 + b * 2 + c
+            remote(mine, place, zs.at[g], zr.at[g], peer).start()
+
+        remote(mine, place, ys.at[g], yr.at[g], mid_peer).start()
+
+    ahead = 3
+
     def greet():
-        own_q.wait()
         pl.semaphore_wait(barrier, n - 1)
 
-        @pl.loop(0, G)
+        @pl.loop(0, ahead)
         def _(g):
-            mine = qall.at[g, c, b, a0, a1]
-
-            @pl.loop(1, A1)
-            def _(k):
-                peer = (lax.rem(a1 + k, A1) * 2 + a0) * 4 + b * 2 + c
-                remote(mine, mine, zs.at[g], zr.at[g], peer).start()
-
-            remote(mine, mine, ys.at[g], yr.at[g], mid_peer).start()
+            send_own(g)
 
         @pl.when(me > 0)
         def _():
@@ -243,6 +247,8 @@
 
     own_rows = pltpu.make_async_copy(rows_send.at[me], rows_out.at[me], ls.at[3])
     own_rows.start()
+    own_q.wait()
+    first, bunch = 4, -(-n // G)
 
     lag = 8
 
@@ -251,6 +257,11 @@
         @pl.when(step < G)
         def _():
             g = step
+
+            @pl.when(g < G - ahead)
+            def _():
+                send_own(g + ahead)
+
             drain(qall.at[g, c, b, a0, pl.ds(0, A1 - 1)], zr.at[g])
             mine = qall.at[g, c, b, a0]
             remote(mine, mine, ws.at[g], wr.at[g], step_peer).start()
@@ -273,12 +284,16 @@
             drain(qall.at[g, c, 1 - b], yr.at[g])
             remote(qall.at[g, c], qall.at[g, c], bs.at[g], br.at[g], core_peer).start()
 
-        @pl.when(step == G + 1)
-        def _():
-            @pl.loop(1, n)
-            def _(k):
-                peer = lax.rem(me + k, n)
-                remote(rows_send.at[peer], rows_out.at[me], rs.at[0], rr.at[0], peer).start()
+        @pl.when((step >= first) & (step < first + G))
+        def _():
+            @pl.loop(0, bunch)
+            def _(i):
+                k = (step - first) * bunch + i
+
+                @pl.when((k > 0) & (k < n))
+                def _():
+                    peer = lax.rem(me + k, n)
+                    remote(rows_send.at[peer], rows_out.at[me], rs.at[0], rr.at[0], peer).start()
 
         @pl.when((step == 5) & (me < n - 1))
         def _():
@@ -361,6 +376,8 @@
         pooled = pooled + pltpu.roll(padded, o, 1) + pltpu.roll(padded, width - o, 1)
     importance = pooled[:, LANES:LANES + positions] * pool_scale
     imp_ref[...] = importance
+    own_imp = pltpu.make_async_copy(imp_ref, imp_out, ls.at[2])
+    own_imp.start()
 
     want, lane = slot_tile[...], slot_lane[...]
     table = jnp.zeros((n, LANES), jnp.float32)
@@ -371,11 +388,13 @@
             table = jnp.where(want == h * tiles + t + 1, found, table)
     for k in range(n):
         ssend[k] = table[k:k + 1, :]
+    own_score = pltpu.make_async_copy(ssend.at[me], score_out.at[me], ls.at[0])
+    own_score.start()
 
     @pl.loop(1, n)
     def _(k):
         peer = lax.rem(me + k, n)
-        remote(ssend.at[peer], srecv.at[me], ss.at[0], sr.at[0], peer).start()
+        remote(ssend.at[peer], score_out.at[me], ss.at[0], sr.at[0], peer).start()
 
     own_rows.wait()
     drain(rows_out.at[pl.ds(0, n - 1)], rr.at[0])
@@ -406,9 +425,9 @@
 
     drain(stat_all.at[pl.ds(0, n - 1)], es.at[0])
     drain(ssend.at[pl.ds(0, n - 1)], ss.at[0])
-    drain(srecv.at[pl.ds(0, n - 1)], sr.at[0])
-    srecv[me] = ssend[me]
-    score_out[...] = srecv[...]
+    own_imp.wait()
+    own_score.wait()
+    drain(score_out.at[pl.ds(0, n - 1)], sr.at[0])
 
 
 def finish(cap, imp_in, rows_in, score_in, imp_ref, rows_ref, score_ref):
@@ -455,7 +474,7 @@
             jax.ShapeDtypeStruct((n, 1, LANES), f32),
         ),
         in_specs=[any_spec] * 6,
-        out_specs=(vmem, any_spec, vmem),
+        out_specs=(any_spec, any_spec, any_spec),
         scratch_shapes=[
             pltpu.VMEM((positions + 2 * EDGE, width), bf16),
             pltpu.VMEM((positions, width), bf16),
@@ -475,7 +494,7 @@
             pltpu.VMEM((KV_HEADS, 1, positions), f32),
             pltpu.VMEM((16 * KV_HEADS, LANES), f32),
             pltpu.VMEM((n, 1, LANES), f32),
-            pltpu.VMEM((n, 1, LANES), f32),
+            pltpu.VMEM((KV_HEADS, positions), f32),
             pltpu.SMEM((1,), jnp.int32),
             pltpu.VMEM((slots,), jnp.int32),
             pltpu.VMEM((slots,), jnp.int32),

time: 51 us -> 45.7 us (0.90)
  Pallas kernels: 49.5 us -> 44.2 us
    pallas_call x1, Pallas kernels: 47.8 us -> 42.5 us  [per_device(): pl.pallas_call(functools.partial(kernel, n, cap, cap_pad, pool_scale), ou...]
where the time goes in v2:
time: 45.7 us; the launch traced here: 45.5 us
  Pallas kernels  44.2 us (97%)
  between operations  1.29 us (3%)
    pallas_call x1, Pallas kernels, per_device(): pl.pallas_call(functools.partial(kernel, n, cap, cap_pad, pool_scale), ou...  42.5 us
    pallas_call x1, Pallas kernels, per_device(): pl.pallas_call(functools.partial(finish, cap), out_shape=(jax.ShapeDtypeS...  1.76 us

profile of v2, /device:TPU:0, one launch (start us, length us, event | category | flops | bytes accessed | tf_op | source)
XLA Modules:
  0.0 45.5 jit_solution(4344585937569269164)
XLA Ops:
  1.3 42.5 %snap.1 = (f32[8,1024]{1,0:T(8,128)}, bf16[16,40,256]{2,1,0:T(8,128)(2,1)}, f32[16,1,128]{2,1,0:T(1,128)}) custom-call(bf16[1024,1024]{1,0:T(8,128)(2,1)} %keys_hbm.1, bf16[1024,1024]{1,0:T(8,128)(2,1)} %vals_hbm.1, bf16[8,64,128]{2,1,0:T(8,128)(2,1)} %bitcast.6, s32[1]{0:T(128)S(6)} %copy.9.count_hbm, s32[640]{0:T(1024)} %entry_hbm.1, s32[640]{0:T(1024)} %owner_hbm.1), custom_call_target="tpu_custom_call" | custom-call | tf_op jit(solution)/shard_map/snap/pallas_call | solution.py:469
  43.8 1.8 %finish.1 = (f32[8,1024]{1,0:T(8,128)}, bf16[16,40,256]{2,1,0:T(8,128)(2,1)}, bf16[640]{0:T(1024)(128)(2,1)}) custom-call(f32[8,1024]{1,0:T(8,128)} %get-tuple-element.9.imp_in, bf16[16,40,256]{2,1,0:T(8,128)(2,1)} %get-tuple-element.10.rows_in, f32[16,1,128]{2,1,0:T(1,128)} %get-tuple-element.11.score_in), custom_call_target="tpu_custom_call" | custom-call | tf_op jit(solution)/shard_map/finish/pallas_call | solution.py:510

commit v3 on v2

v3 whole, which is shorter than its diff:
```python
import functools

import jax
import jax.numpy as jnp
from jax import lax
from jax.experimental import pallas as pl
from jax.experimental.pallas import tpu as pltpu
from jax.sharding import PartitionSpec as P

KV_HEADS = 8
GROUP = 8
HEAD_DIM = 128
POOL = 7
LOG2E = 1.4426950408889634
LANES = 128
EDGE = 16
STRIP = 64
HALVES = 2
MESH = pl.DeviceIdType.MESH
NT = (((1,), (1,)), ((), ()))


def iota(shape, dim):
    return lax.broadcasted_iota(jnp.int32, shape, dim)


def kernel(
    n, cap, cap_pad, pool_scale,
    keys_hbm, vals_hbm, wq_hbm, count_hbm, entry_hbm, owner_hbm,
    imp_out, rows_out, score_out,
    keys, vals, qall, ebuf, raw, peak, sums, macc, stat, stat_x, stat_z, rows_send, onehot, slot_tile, slot_lane,
    mass, edge, ssend, imp_ref, count_ref, entry_ref, owner_ref,
    zs, zr, ws, wr, ys, yr, bs, br, xs, xr, qs, qr, rs, rr, hs, hr, ss, sr, ls,
):
    G = KV_HEADS
    me = lax.axis_index("seq")
    A = n // 4
    N, U = qall.shape[1], qall.shape[4]
    H = G // HALVES
    units = N * HALVES
    relay = U == 1 and N == 4
    a, b, c = me // 4, (me // 2) % 2, me % 2
    inner = a % U

    mine = a // U
    slots = entry_ref.shape[0]
    positions = vals.shape[0]
    tiles = positions // LANES
    out_slots = n * cap_pad
    chunk = ebuf.shape[3]
    scale2 = HEAD_DIM ** (-0.5) * LOG2E
    quad = b * 2 + c

    def to(index):
        return {"seq": index}

    def remote(src, dst, ssem, rsem, index):
        return pltpu.make_async_remote_copy(
            src_ref=src, dst_ref=dst, send_sem=ssem, recv_sem=rsem,
            device_id=to(index), device_id_type=MESH,
        )

    def drain(region, sem):
        pltpu.make_async_copy(region, region, sem).wait()

    low, high = lax.rem(me + n - 1, n), lax.rem(me + 1, n)
    mid_peer = a * 4 + (1 - b) * 2 + c
    core_peer = a * 4 + b * 2 + (1 - c)
    near, across = a + 1 - 2 * (a % 2), (a + 2) % A

    def hop_of(p):
        return jnp.where(a < 2, jnp.where(p == 0, 0, jnp.where(p == 3, 1, p + 1)), p)

    def unit_at(p):
        if not relay:
            return lax.rem(mine + p, N)
        hop = hop_of(p)
        return jnp.where(hop == 0, a, jnp.where(hop == 1, near, jnp.where(hop == 2, across, A - 1 - a)))

    def joined_at(p):
        return jnp.where(p < 2, p + 2, 3 - p) if relay else p


    def line_peer(k):
        return lax.rem(a + k, A) * 4 + b * 2 + c

    barrier = pltpu.get_barrier_semaphore()

    def announce(index):
        pl.semaphore_signal(barrier, inc=1, device_id=to(index), device_id_type=MESH)

    @pl.loop(1, A)
    def _(k):
        announce(line_peer(k))

    announce(mid_peer)
    announce(core_peer)

    @pl.when(me > 0)
    def _():
        announce(low)

    @pl.when(me < n - 1)
    def _():
        announce(high)

    own_q = pltpu.make_async_copy(wq_hbm, qall.at[:, mine, c, b, inner], ls.at[2])
    small = [
        pltpu.make_async_copy(src, dst, ls.at[4 + i])
        for i, (src, dst) in enumerate(((count_hbm, count_ref), (entry_hbm, entry_ref), (owner_hbm, owner_ref)))
    ]
    key_copy = pltpu.make_async_copy(keys_hbm, keys.at[pl.ds(0, positions)], ls.at[0])
    val_copy = pltpu.make_async_copy(vals_hbm, vals, ls.at[1])
    own_q.start()
    for copy in small:
        copy.start()
    key_copy.start()
    val_copy.start()

    first_rows = pl.ds(0, EDGE)
    last_rows = pl.ds(positions - EDGE, EDGE)
    from_low = pl.ds(positions, EDGE)
    from_high = pl.ds(positions + EDGE, EDGE)

    @pl.when(me == 0)
    def _():
        keys[positions:positions + EDGE, :] = jnp.zeros((EDGE, keys.shape[1]), keys.dtype)

    @pl.when(me == n - 1)
    def _():
        keys[positions + EDGE:positions + 2 * EDGE, :] = jnp.zeros((EDGE, keys.shape[1]), keys.dtype)

    def half(h):
        return pl.ds(h * H, H)

    def pieces(count):
        return qall.at[half(0)].reshape(H * N * 4 * U, qall.shape[5], HEAD_DIM).at[pl.ds(0, H * count)]

    def on_line(index):
        return index * 4 + b * 2 + c

    def greet():
        ends = jnp.where(me > 0, 1, 0) + jnp.where(me < n - 1, 1, 0)
        pl.semaphore_wait(barrier, A + 1 + ends)

        @pl.loop(0, HALVES)
        def _(h):
            piece, place, k = wq_hbm.at[half(h)], qall.at[half(h), mine, c, b, inner], mine * HALVES + h

            def send(index):
                remote(piece, place, zs.at[h], zr.at[k], on_line(index)).start()

            if relay:
                send(near)
                send(across)
            else:
                @pl.loop(1, A)
                def _(i):
                    send(lax.rem(a + i, A))

        own_q.wait()
        if U == 1:
            @pl.loop(0, HALVES)
            def _(h):
                block = qall.at[half(h), mine, c, b]
                remote(block, block, ys.at[mine * HALVES + h], yr.at[mine * HALVES + h], mid_peer).start()

        @pl.when(me > 0)
        def _():
            remote(keys_hbm.at[first_rows], keys.at[from_high], hs.at[0], hr.at[0], low).start()

        @pl.when(me < n - 1)
        def _():
            remote(keys_hbm.at[last_rows], keys.at[from_low], hs.at[1], hr.at[1], high).start()

    reach = a + b
    late = reach > A // 2

    @pl.when(late)
    def _():
        greet()

    for copy in small:
        copy.wait()
    entry = entry_ref[...].reshape(1, slots)
    owner = owner_ref[...].reshape(1, slots)
    live = iota((1, slots), 1) < count_ref[0]
    owner_live = jnp.where(live, owner, -1)
    member = jnp.where(iota((n, slots), 0) == owner_live, 1.0, 0.0)
    before = jnp.where(iota((slots, slots), 0) < iota((slots, slots), 1), 1.0, 0.0).astype(jnp.bfloat16)
    earlier = jnp.dot(member.astype(jnp.bfloat16), before, preferred_element_type=jnp.float32)
    rank = jnp.sum(member * earlier, axis=0, keepdims=True).astype(jnp.int32)
    target = jnp.where(live, owner * cap_pad + rank, -1)
    tile_of = entry // LANES
    lane_of = entry - tile_of * LANES
    head = tile_of // tiles
    token_f = (entry - head * positions + 1).astype(jnp.float32)
    head_f = head.astype(jnp.float32)
    at_rank = jnp.where(iota((LANES, slots), 0) == rank, 1.0, 0.0).astype(jnp.bfloat16)

    def by_rank(value):
        marked = (member * value.astype(jnp.float32)).astype(jnp.bfloat16)
        return lax.dot_general(marked, at_rank, NT, preferred_element_type=jnp.float32).astype(jnp.int32)

    slot_tile[...] = by_rank(tile_of + 1)
    slot_lane[...] = by_rank(lane_of)

    @pl.when(reach == A // 2)
    def _():
        greet()

    key_copy.wait()
    val_copy.wait()

    def gather_rows(k0, count):
        blk = count * cap_pad
        hit = (iota((blk, slots), 0) + k0 * cap_pad) == target
        tok = jnp.sum(jnp.where(hit, token_f, 0.0), axis=1, keepdims=True).astype(jnp.int32) - 1
        hcol = jnp.sum(jnp.where(hit, head_f, 0.0), axis=1, keepdims=True).astype(jnp.int32)
        hcol = jnp.broadcast_to(hcol, (blk, HEAD_DIM))
        onehot[...] = jnp.where(iota((blk, positions), 1) == tok, 1.0, 0.0).astype(jnp.bfloat16)
        for side, source in enumerate((keys, vals)):
            got = jnp.dot(onehot[...], source[0:positions, :], preferred_element_type=jnp.float32)
            chosen = jnp.zeros((blk, HEAD_DIM), jnp.float32)
            for h in range(G):
                chosen = jnp.where(hcol == h, got[:, h * HEAD_DIM:(h + 1) * HEAD_DIM], chosen)
            for k in range(count):
                rows_send[k0 + k, :, side * HEAD_DIM:(side + 1) * HEAD_DIM] = chosen[
                    k * cap_pad:(k + 1) * cap_pad
                ].astype(jnp.bfloat16)

    per = onehot.shape[0] // cap_pad
    gather_rows(0, per)

    @pl.when(reach < A // 2)
    def _():
        greet()

    def lse(values):
        top = values[0]
        for x in values[1:]:
            top = jnp.maximum(top, x)
        total = jnp.zeros_like(top)
        for x in values:
            total = total + jnp.exp2(x - top)
        return top + jnp.log(total) * LOG2E

    def join_quad(i):
        g = unit_at(i // HALVES) * HALVES + i % HALVES
        drain(stat_x.at[g, pl.ds(0, 3)], xr.at[g])
        stat_z[g, a] = lse([stat_x[g, d] for d in range(4)])

        @pl.loop(1, A)
        def _(k):
            peer = lax.rem(a + k, A) * 4 + quad
            remote(stat_z.at[g, a], stat_z.at[g, a], qs.at[g], qr.at[g], peer).start()

    strip = sums.shape[1]
    span = positions // strip
    columns = chunk // LANES

    def compute(r, h):
        k = r * HALVES + h
        for i in range(H):
            g = h * H + i
            group_q = qall.at[g, r].reshape(chunk, HEAD_DIM)
            key_cols = pl.ds(pl.multiple_of(g * HEAD_DIM, HEAD_DIM), HEAD_DIM)
            s = lax.dot_general(keys[:, key_cols], group_q[...], NT, preferred_element_type=jnp.float32)
            for u in range(strip):
                x = s[u * span:(u + 1) * span].reshape(span // 8, 8, chunk)
                top = jnp.max(x, axis=0)
                e = jnp.exp2((x - top[None]) * scale2)
                ebuf[k, i, u * span:(u + 1) * span, :] = e.reshape(span, chunk)
                peak[k, i, u] = top
                sums[i, u] = jnp.sum(e, axis=0)
            raw[k, i, 0:8, :] = s[positions + EDGE - 8:positions + EDGE]
            raw[k, i, 8:16, :] = s[positions + EDGE:positions + EDGE + 8]
        for i in range(H):
            tops = peak[k, i]
            top = jnp.max(jnp.max(tops, axis=0), axis=0, keepdims=True)
            total = jnp.sum(jnp.sum(sums[i] * jnp.exp2((tops - top[None]) * scale2), axis=0), axis=0, keepdims=True)
            local = top * scale2 + jnp.log(total) * LOG2E
            for j in range(columns):
                stat[k, i * columns + j:i * columns + j + 1, :] = local[:, j * LANES:(j + 1) * LANES]
        stat_x[k, quad] = stat[k]

        @pl.loop(1, 4)
        def _(d):
            peer = a * 4 + lax.rem(quad + d, 4)
            remote(stat.at[k], stat_x.at[k, quad], xs.at[k], xr.at[k], peer).start()

    own_rows = pltpu.make_async_copy(rows_send.at[me], rows_out.at[me], ls.at[3])
    lag = 3

    @pl.loop(0, G)
    def _(g):
        macc[g] = jnp.zeros(macc.shape[1:], jnp.float32)

    edge[...] = jnp.zeros(edge.shape, jnp.float32)

    def send_middle(i):
        p, h = i // HALVES, i % HALVES
        unit = unit_at(p)
        k = unit * HALVES + h
        block = qall.at[half(h), unit, c, b]

        @pl.when(p > 0)
        def _():
            drain(pieces(U), zr.at[k])

        if U > 1:
            @pl.when(p == 0)
            def _():
                drain(pieces(U - 1), zr.at[k])

            remote(block, block, ys.at[k], yr.at[k], mid_peer).start()
        else:
            @pl.when(p > 0)
            def _():
                remote(block, block, ys.at[k], yr.at[k], mid_peer).start()

        if relay:
            @pl.when(hop_of(p) == 2)
            def _():
                remote(block, block, ws.at[h], zr.at[k], on_line(near)).start()

    def send_core(i):
        h = i % HALVES
        unit = unit_at(i // HALVES)
        k = unit * HALVES + h
        drain(qall.at[half(h), unit, c, 1 - b], yr.at[k])
        block = qall.at[half(h), unit, c]
        remote(block, block, bs.at[k], br.at[k], core_peer).start()

    if U > 1:
        for i in range(HALVES):
            send_middle(i)

    @pl.loop(0, units + 1)
    def _(step):
        @pl.when((step > 0) & (step < units - 2))
        def _():
            send_middle(step + 2)

        @pl.when(step < units)
        def _():
            send_core(step)

        @pl.when(step == 0)
        def _():
            gather_rows(per, per)
            own_rows.start()
            send_middle(step + 2)

        @pl.when((step == 1) & (me < n - 1))
        def _():
            drain(keys.at[from_high], hr.at[0])

        @pl.when((step == 1) & (me > 0))
        def _():
            drain(keys.at[from_low], hr.at[1])

        @pl.when(step >= 1)
        def _():
            h = (step - 1) % HALVES
            unit = unit_at((step - 1) // HALVES)
            drain(qall.at[half(h), unit, 1 - c], br.at[unit * HALVES + h])
            compute(unit, h)

        @pl.when(step >= lag)
        def _():
            join_quad(step - lag)

    join_quad(units - 2)
    join_quad(units - 1)

    @pl.loop(1, n)
    def _(k):
        peer = lax.rem(me + k, n)
        remote(rows_send.at[peer], rows_out.at[me], rs.at[0], rr.at[0], peer).start()

    @pl.loop(0, units)
    def _(i):
        h = i % HALVES
        k = joined_at(i // HALVES) * HALVES + h
        drain(stat_z.at[k, pl.ds(0, A - 1)], qr.at[k])
        whole = lse([stat_z[k, d] for d in range(A)])
        for j in range(H):
            g = h * H + j
            level = [whole[j * columns + d:j * columns + d + 1, :] for d in range(columns)]
            for u in range(strip):
                weight = [
                    jnp.exp2(peak[k, j, u, :, d * LANES:(d + 1) * LANES] * scale2 - level[d]) for d in range(columns)
                ]
                rows = slice(u * span, (u + 1) * span)
                acc = macc[g, rows, :].reshape(span // 8, 8, LANES)
                for d in range(columns):
                    e = ebuf[k, j, rows, d * LANES:(d + 1) * LANES].reshape(span // 8, 8, LANES)
                    acc = acc + e * weight[d][None]
                macc[g, rows, :] = acc.reshape(span, LANES)
            acc = edge[pl.ds(pl.multiple_of(g * 16, 16), 16), :]
            for d in range(columns):
                acc = acc + jnp.exp2(raw[k, j, :, d * LANES:(d + 1) * LANES] * scale2 - level[d])
            edge[pl.ds(pl.multiple_of(g * 16, 16), 16), :] = acc

        @pl.when(i >= units - HALVES)
        def _():
            for j in range(H):
                g = h * H + j
                for t in range(tiles):
                    acc = macc[g, t * LANES:(t + 1) * LANES, :]
                    mass[g, :, t * LANES:(t + 1) * LANES] = jnp.sum(acc.T, axis=0, keepdims=True)

    column = jnp.concatenate([mass[g] for g in range(G)], axis=0)
    line = jnp.sum(edge[...].T, axis=0, keepdims=True)
    row_of = iota((G, LANES), 0)
    ends = jnp.zeros((G, LANES), jnp.float32)
    for g in range(G):
        turned = pltpu.roll(line, (LANES - 8 - 16 * g) % LANES, 1)
        ends = jnp.where(row_of == g, turned, ends)
    before_low = jnp.where(me > 0, ends, 0.0)
    after_high = jnp.where(me < n - 1, ends, 0.0)
    padded = jnp.concatenate([before_low, column, after_high], axis=1)
    width = padded.shape[1]
    pooled = padded
    for o in range(1, POOL // 2 + 1):
        pooled = pooled + pltpu.roll(padded, o, 1) + pltpu.roll(padded, width - o, 1)
    importance = pooled[:, LANES:LANES + positions] * pool_scale
    imp_ref[...] = importance
    own_imp = pltpu.make_async_copy(imp_ref, imp_out, ls.at[2])
    own_imp.start()

    want, lane = slot_tile[...], slot_lane[...]
    table = jnp.zeros((n, LANES), jnp.float32)
    for h in range(G):
        for t in range(tiles):
            part = jnp.broadcast_to(importance[h:h + 1, t * LANES:(t + 1) * LANES], (n, LANES))
            found = jnp.take_along_axis(part, lane, axis=1)
            table = jnp.where(want == h * tiles + t + 1, found, table)
    for k in range(n):
        ssend[k] = table[k:k + 1, :]
    own_score = pltpu.make_async_copy(ssend.at[me], score_out.at[me], ls.at[0])
    own_score.start()

    @pl.loop(1, n)
    def _(k):
        peer = lax.rem(me + k, n)
        remote(ssend.at[peer], score_out.at[me], ss.at[0], sr.at[0], peer).start()

    own_rows.wait()
    drain(rows_out.at[pl.ds(0, n - 1)], rr.at[0])
    drain(rows_send.at[pl.ds(0, n - 1)], rs.at[0])

    @pl.loop(0, HALVES)
    def _(h):
        if relay:
            drain(pieces(2), zs.at[h])
            drain(pieces(1), ws.at[h])
        else:
            drain(pieces(A - 1), zs.at[h])

    @pl.loop(0, units)
    def _(k):
        r, h = k // HALVES, k % HALVES
        drain(qall.at[half(h), r, c, b], ys.at[k])
        drain(qall.at[half(h), r, c], bs.at[k])
        drain(stat_x.at[k, pl.ds(0, 3)], xs.at[k])
        drain(stat_z.at[k, pl.ds(0, A - 1)], qs.at[k])

    @pl.when(me > 0)
    def _():
        drain(keys.at[from_high], hs.at[0])

    @pl.when(me < n - 1)
    def _():
        drain(keys.at[from_low], hs.at[1])

    drain(ssend.at[pl.ds(0, n - 1)], ss.at[0])
    own_imp.wait()
    own_score.wait()
    drain(score_out.at[pl.ds(0, n - 1)], sr.at[0])


def finish(cap, imp_in, rows_in, score_in, imp_ref, rows_ref, score_ref):
    n = rows_in.shape[0]
    imp_ref[...] = imp_in[...]
    rows_ref[...] = rows_in[:, 0:cap, :]
    table = jnp.concatenate([score_in[k] for k in range(n)], axis=0).astype(jnp.bfloat16)
    column = iota((LANES, n * cap), 1) - iota((LANES, n * cap), 0)
    unfold = jnp.where(column % cap == 0, 1.0, 0.0)
    unfold = jnp.where(iota((LANES, n * cap), 0) < cap, unfold, 0.0).astype(jnp.bfloat16)
    wide = jnp.dot(table, unfold, preferred_element_type=jnp.float32)
    within = iota((n, n * cap), 1) - iota((n, n * cap), 0) * cap
    line = jnp.sum(jnp.where((within >= 0) & (within < cap), wide, 0.0), axis=0, keepdims=True)
    score_ref[...] = line.astype(jnp.bfloat16).reshape(n * cap)


def per_device(n, cached_keys, cached_values, window_queries, kept_count, kept_entry, row_owner):
    positions, width = cached_keys.shape
    slots = kept_entry.shape[0]
    cap = slots // n
    cap_pad = -(-cap // 8) * 8
    query_rows = window_queries.shape[0]
    heads = window_queries.shape[1] // HEAD_DIM
    group = heads // KV_HEADS
    window = query_rows * n
    qrows = query_rows * group
    chunk = 2 * LANES
    slots_q = n * qrows // chunk
    units = slots_q * HALVES
    lane_rows = KV_HEADS // HALVES * chunk // LANES
    wq = (
        window_queries.reshape(query_rows, heads, HEAD_DIM)
        .transpose(1, 0, 2)
        .reshape(KV_HEADS, qrows, HEAD_DIM)
    )
    pool_scale = n * positions / (group * window * POOL)
    any_spec = pl.BlockSpec(memory_space=pl.ANY)
    vmem = pl.BlockSpec(memory_space=pltpu.VMEM)
    dma = pltpu.SemaphoreType.DMA
    A = n // 4
    f32, bf16 = jnp.float32, jnp.bfloat16
    importance, rows, score = pl.pallas_call(
        functools.partial(kernel, n, cap, cap_pad, pool_scale),
        out_shape=(
            jax.ShapeDtypeStruct((KV_HEADS, positions), f32),
            jax.ShapeDtypeStruct((n, cap_pad, 2 * HEAD_DIM), bf16),
            jax.ShapeDtypeStruct((n, 1, LANES), f32),
        ),
        in_specs=[any_spec] * 6,
        out_specs=(any_spec, any_spec, any_spec),
        scratch_shapes=[
            pltpu.VMEM((positions + 2 * EDGE, width), bf16),
            pltpu.VMEM((positions, width), bf16),
            pltpu.VMEM((KV_HEADS, slots_q, 2, 2, A // slots_q, qrows, HEAD_DIM), bf16),
            pltpu.VMEM((units, KV_HEADS // HALVES, positions, chunk), f32),
            pltpu.VMEM((units, KV_HEADS // HALVES, 16, chunk), f32),
            pltpu.VMEM((units, KV_HEADS // HALVES, positions // STRIP, 8, chunk), f32),
            pltpu.VMEM((KV_HEADS // HALVES, positions // STRIP, 8, chunk), f32),
            pltpu.VMEM((KV_HEADS, positions, LANES), f32),
            pltpu.VMEM((units, lane_rows, LANES), f32),
            pltpu.VMEM((units, 4, lane_rows, LANES), f32),
            pltpu.VMEM((units, n // 4, lane_rows, LANES), f32),
            pltpu.VMEM((n, cap_pad, 2 * HEAD_DIM), bf16),
            pltpu.VMEM((n * cap_pad // 2, positions), bf16),
            pltpu.VMEM((n, LANES), jnp.int32),
            pltpu.VMEM((n, LANES), jnp.int32),
            pltpu.VMEM((KV_HEADS, 1, positions), f32),
            pltpu.VMEM((16 * KV_HEADS, LANES), f32),
            pltpu.VMEM((n, 1, LANES), f32),
            pltpu.VMEM((KV_HEADS, positions), f32),
            pltpu.SMEM((1,), jnp.int32),
            pltpu.VMEM((slots,), jnp.int32),
            pltpu.VMEM((slots,), jnp.int32),
        ]
        + [dma((units,))] * 12
        + [dma((1,)), dma((1,)), dma((2,)), dma((2,)), dma((1,)), dma((1,)), dma((7,))],
        compiler_params=pltpu.CompilerParams(
            collective_id=0, has_side_effects=True, vmem_limit_bytes=60 * 1024 * 1024
        ),
        name="snap",
    )(cached_keys, cached_values, wq, kept_count, kept_entry, row_owner)
    importance, rows, score = pl.pallas_call(
        functools.partial(finish, cap),
        out_shape=(
            jax.ShapeDtypeStruct((KV_HEADS, positions), f32),
            jax.ShapeDtypeStruct((n, cap, 2 * HEAD_DIM), bf16),
            jax.ShapeDtypeStruct((n * cap,), bf16),
        ),
        in_specs=[vmem, vmem, vmem],
        out_specs=(vmem, vmem, vmem),
        name="finish",
    )(importance, rows, score)
    return importance, rows.reshape(n * cap, 2 * HEAD_DIM), score


def solution(mesh):
    n = mesh.shape["seq"]
    split = P(("rep", "seq"))
    wide = P(("rep", "seq"), None)
    return jax.shard_map(
        functools.partial(per_device, n),
        mesh=mesh,
        in_specs=(wide, wide, wide, split, split, split),
        out_specs=(P("rep", "seq"), wide, split),
        check_vma=False,
    )
```

time: 45.7 us -> 44.6 us (0.976)
  Pallas kernels: 44.2 us -> 43.2 us
    pallas_call x1, Pallas kernels: 42.5 us -> 41.4 us  [per_device(): pl.pallas_call(functools.partial(kernel, n, cap, cap_pad, pool_scale), ou...]
where the time goes in v3:
time: 44.6 us; the launch traced here: 44.5 us
  Pallas kernels  43.2 us (97%)
  between operations  1.29 us (3%)
    pallas_call x1, Pallas kernels, per_device(): pl.pallas_call(functools.partial(kernel, n, cap, cap_pad, pool_scale), ou...  41.4 us
    pallas_call x1, Pallas kernels, per_device(): pl.pallas_call(functools.partial(finish, cap), out_shape=(jax.ShapeDtypeS...  1.76 us

profile of v3, /device:TPU:0, one launch (start us, length us, event | category | flops | bytes accessed | tf_op | source)
XLA Modules:
  0.0 44.5 jit_solution(5140090437413353663)
XLA Ops:
  1.3 41.4 %snap.1 = (f32[8,1024]{1,0:T(8,128)}, bf16[16,40,256]{2,1,0:T(8,128)(2,1)}, f32[16,1,128]{2,1,0:T(1,128)}) custom-call(bf16[1024,1024]{1,0:T(8,128)(2,1)} %keys_hbm.1, bf16[1024,1024]{1,0:T(8,128)(2,1)} %vals_hbm.1, bf16[8,64,128]{2,1,0:T(8,128)(2,1)} %bitcast.6, s32[1]{0:T(128)S(6)} %copy.9.count_hbm, s32[640]{0:T(1024)} %entry_hbm.1, s32[640]{0:T(1024)} %owner_hbm.1), custom_call_target="tpu_custom_call" | custom-call | tf_op jit(solution)/shard_map/snap/pallas_call | solution.py:523
  42.7 1.8 %finish.1 = (f32[8,1024]{1,0:T(8,128)}, bf16[16,40,256]{2,1,0:T(8,128)(2,1)}, bf16[640]{0:T(1024)(128)(2,1)}) custom-call(f32[8,1024]{1,0:T(8,128)} %get-tuple-element.9.imp_in, bf16[16,40,256]{2,1,0:T(8,128)(2,1)} %get-tuple-element.10.rows_in, f32[16,1,128]{2,1,0:T(1,128)} %get-tuple-element.11.score_in), custom_call_target="tpu_custom_call" | custom-call | tf_op jit(solution)/shard_map/finish/pallas_call | solution.py:563

commit v4 on v3

--- a/solution.py
+++ b/solution.py
@@ -49,8 +49,6 @@
     out_slots = n * cap_pad
     chunk = ebuf.shape[3]
     scale2 = HEAD_DIM ** (-0.5) * LOG2E
-    quad = b * 2 + c
-
     def to(index):
         return {"seq": index}
 
@@ -143,6 +141,12 @@
         ends = jnp.where(me > 0, 1, 0) + jnp.where(me < n - 1, 1, 0)
         pl.semaphore_wait(barrier, A + 1 + ends)
 
+        if U == 1:
+            @pl.loop(0, HALVES)
+            def _(h):
+                k = mine * HALVES + h
+                remote(wq_hbm.at[half(h)], qall.at[half(h), mine, c, b, inner], ys.at[k], yr.at[k], mid_peer).start()
+
         @pl.loop(0, HALVES)
         def _(h):
             piece, place, k = wq_hbm.at[half(h)], qall.at[half(h), mine, c, b, inner], mine * HALVES + h
@@ -157,13 +161,6 @@
                 @pl.loop(1, A)
                 def _(i):
                     send(lax.rem(a + i, A))
-
-        own_q.wait()
-        if U == 1:
-            @pl.loop(0, HALVES)
-            def _(h):
-                block = qall.at[half(h), mine, c, b]
-                remote(block, block, ys.at[mine * HALVES + h], yr.at[mine * HALVES + h], mid_peer).start()
 
         @pl.when(me > 0)
         def _():
@@ -245,15 +242,18 @@
             total = total + jnp.exp2(x - top)
         return top + jnp.log(total) * LOG2E
 
-    def join_quad(i):
+    chips = n // 2
+    chip = me // 2
+
+    def join_pair(i):
         g = unit_at(i // HALVES) * HALVES + i % HALVES
-        drain(stat_x.at[g, pl.ds(0, 3)], xr.at[g])
-        stat_z[g, a] = lse([stat_x[g, d] for d in range(4)])
-
-        @pl.loop(1, A)
+        drain(stat_x.at[g, pl.ds(0, 1)], xr.at[g])
+        stat_z[g, chip] = lse([stat_x[g, d] for d in range(2)])
+
+        @pl.loop(1, chips)
         def _(k):
-            peer = lax.rem(a + k, A) * 4 + quad
-            remote(stat_z.at[g, a], stat_z.at[g, a], qs.at[g], qr.at[g], peer).start()
+            peer = lax.rem(chip + k, chips) * 2 + c
+            remote(stat_z.at[g, chip], stat_z.at[g, chip], qs.at[g], qr.at[g], peer).start()
 
     strip = sums.shape[1]
     span = positions // strip
@@ -282,15 +282,11 @@
             local = top * scale2 + jnp.log(total) * LOG2E
             for j in range(columns):
                 stat[k, i * columns + j:i * columns + j + 1, :] = local[:, j * LANES:(j + 1) * LANES]
-        stat_x[k, quad] = stat[k]
-
-        @pl.loop(1, 4)
-        def _(d):
-            peer = a * 4 + lax.rem(quad + d, 4)
-            remote(stat.at[k], stat_x.at[k, quad], xs.at[k], xr.at[k], peer).start()
+        stat_x[k, c] = stat[k]
+        remote(stat.at[k], stat_x.at[k, c], xs.at[k], xr.at[k], core_peer).start()
 
     own_rows = pltpu.make_async_copy(rows_send.at[me], rows_out.at[me], ls.at[3])
-    lag = 3
+    lag = 2
 
     @pl.loop(0, G)
     def _(g):
@@ -332,24 +328,28 @@
         block = qall.at[half(h), unit, c]
         remote(block, block, bs.at[k], br.at[k], core_peer).start()
 
+    own_q.wait()
     if U > 1:
         for i in range(HALVES):
             send_middle(i)
 
     @pl.loop(0, units + 1)
     def _(step):
-        @pl.when((step > 0) & (step < units - 2))
-        def _():
-            send_middle(step + 2)
-
-        @pl.when(step < units)
-        def _():
-            send_core(step)
-
         @pl.when(step == 0)
         def _():
             gather_rows(per, per)
             own_rows.start()
+
+        @pl.when((step > 0) & (step < units - 2))
+        def _():
+            send_middle(step + 2)
+
+        @pl.when(step < units)
+        def _():
+            send_core(step)
+
+        @pl.when(step == 0)
+        def _():
             send_middle(step + 2)
 
         @pl.when((step == 1) & (me < n - 1))
@@ -369,10 +369,9 @@
 
         @pl.when(step >= lag)
         def _():
-            join_quad(step - lag)
-
-    join_quad(units - 2)
-    join_quad(units - 1)
+            join_pair(step - lag)
+
+    join_pair(units - 1)
 
     @pl.loop(1, n)
     def _(k):
@@ -383,8 +382,8 @@
     def _(i):
         h = i % HALVES
         k = joined_at(i // HALVES) * HALVES + h
-        drain(stat_z.at[k, pl.ds(0, A - 1)], qr.at[k])
-        whole = lse([stat_z[k, d] for d in range(A)])
+        drain(stat_z.at[k, pl.ds(0, chips - 1)], qr.at[k])
+        whole = lse([stat_z[k, d] for d in range(chips)])
         for j in range(H):
             g = h * H + j
             level = [whole[j * columns + d:j * columns + d + 1, :] for d in range(columns)]
@@ -464,8 +463,8 @@
         r, h = k // HALVES, k % HALVES
         drain(qall.at[half(h), r, c, b], ys.at[k])
         drain(qall.at[half(h), r, c], bs.at[k])
-        drain(stat_x.at[k, pl.ds(0, 3)], xs.at[k])
-        drain(stat_z.at[k, pl.ds(0, A - 1)], qs.at[k])
+        drain(stat_x.at[k, pl.ds(0, 1)], xs.at[k])
+        drain(stat_z.at[k, pl.ds(0, chips - 1)], qs.at[k])
 
     @pl.when(me > 0)
     def _():
@@ -539,8 +538,8 @@
             pltpu.VMEM((KV_HEADS // HALVES, positions // STRIP, 8, chunk), f32),
             pltpu.VMEM((KV_HEADS, positions, LANES), f32),
             pltpu.VMEM((units, lane_rows, LANES), f32),
-            pltpu.VMEM((units, 4, lane_rows, LANES), f32),
-            pltpu.VMEM((units, n // 4, lane_rows, LANES), f32),
+            pltpu.VMEM((units, 2, lane_rows, LANES), f32),
+            pltpu.VMEM((units, n // 2, lane_rows, LANES), f32),
             pltpu.VMEM((n, cap_pad, 2 * HEAD_DIM), bf16),
             pltpu.VMEM((n * cap_pad // 2, positions), bf16),
             pltpu.VMEM((n, LANES), jnp.int32),

time: 44.6 us -> 44.1 us (0.989)
  Pallas kernels: 43.2 us -> 42.6 us
    pallas_call x1, Pallas kernels: 41.4 us -> 40.9 us  [per_device(): pl.pallas_call(functools.partial(kernel, n, cap, cap_pad, pool_scale), ou...]
where the time goes in v4:
time: 44.1 us; the launch traced here: 43.9 us
  Pallas kernels  42.6 us (97%)
  between operations  1.29 us (3%)
    pallas_call x1, Pallas kernels, per_device(): pl.pallas_call(functools.partial(kernel, n, cap, cap_pad, pool_scale), ou...  40.9 us
    pallas_call x1, Pallas kernels, per_device(): pl.pallas_call(functools.partial(finish, cap), out_shape=(jax.ShapeDtypeS...  1.76 us

profile of v4, /device:TPU:0, one launch (start us, length us, event | category | flops | bytes accessed | tf_op | source)
XLA Modules:
  0.0 43.9 jit_solution(11943599852525310436)
XLA Ops:
  1.3 40.9 %snap.1 = (f32[8,1024]{1,0:T(8,128)}, bf16[16,40,256]{2,1,0:T(8,128)(2,1)}, f32[16,1,128]{2,1,0:T(1,128)}) custom-call(bf16[1024,1024]{1,0:T(8,128)(2,1)} %keys_hbm.1, bf16[1024,1024]{1,0:T(8,128)(2,1)} %vals_hbm.1, bf16[8,64,128]{2,1,0:T(8,128)(2,1)} %bitcast.6, s32[1]{0:T(128)S(6)} %copy.9.count_hbm, s32[640]{0:T(1024)} %entry_hbm.1, s32[640]{0:T(1024)} %owner_hbm.1), custom_call_target="tpu_custom_call" | custom-call | tf_op jit(solution)/shard_map/snap/pallas_call | solution.py:522
  42.2 1.8 %finish.1 = (f32[8,1024]{1,0:T(8,128)}, bf16[16,40,256]{2,1,0:T(8,128)(2,1)}, bf16[640]{0:T(1024)(128)(2,1)}) custom-call(f32[8,1024]{1,0:T(8,128)} %get-tuple-element.9.imp_in, bf16[16,40,256]{2,1,0:T(8,128)(2,1)} %get-tuple-element.10.rows_in, f32[16,1,128]{2,1,0:T(1,128)} %get-tuple-element.11.score_in), custom_call_target="tpu_custom_call" | custom-call | tf_op jit(solution)/shard_map/finish/pallas_call | solution.py:562

commit v5 on v4

--- a/solution.py
+++ b/solution.py
@@ -16,6 +16,7 @@
 EDGE = 16
 STRIP = 64
 HALVES = 2
+FAR_STEP = -1
 MESH = pl.DeviceIdType.MESH
 NT = (((1,), (1,)), ((), ()))
 
@@ -145,14 +146,14 @@
             @pl.loop(0, HALVES)
             def _(h):
                 k = mine * HALVES + h
-                remote(wq_hbm.at[half(h)], qall.at[half(h), mine, c, b, inner], ys.at[k], yr.at[k], mid_peer).start()
+                remote(wq_hbm.at[half(h)], qall.at[half(h), mine, c, b, inner], ys.at[0], yr.at[k], mid_peer).start()
 
         @pl.loop(0, HALVES)
         def _(h):
             piece, place, k = wq_hbm.at[half(h)], qall.at[half(h), mine, c, b, inner], mine * HALVES + h
 
             def send(index):
-                remote(piece, place, zs.at[h], zr.at[k], on_line(index)).start()
+                remote(piece, place, zs.at[0], zr.at[k], on_line(index)).start()
 
             if relay:
                 send(near)
@@ -253,7 +254,7 @@
         @pl.loop(1, chips)
         def _(k):
             peer = lax.rem(chip + k, chips) * 2 + c
-            remote(stat_z.at[g, chip], stat_z.at[g, chip], qs.at[g], qr.at[g], peer).start()
+            remote(stat_z.at[g, chip], stat_z.at[g, chip], qs.at[0], qr.at[g], peer).start()
 
     strip = sums.shape[1]
     span = positions // strip
@@ -283,7 +284,7 @@
             for j in range(columns):
                 stat[k, i * columns + j:i * columns + j + 1, :] = local[:, j * LANES:(j + 1) * LANES]
         stat_x[k, c] = stat[k]
-        remote(stat.at[k], stat_x.at[k, c], xs.at[k], xr.at[k], core_peer).start()
+        remote(stat.at[k], stat_x.at[k, c], xs.at[0], xr.at[k], core_peer).start()
 
     own_rows = pltpu.make_async_copy(rows_send.at[me], rows_out.at[me], ls.at[3])
     lag = 2
@@ -309,16 +310,16 @@
             def _():
                 drain(pieces(U - 1), zr.at[k])
 
-            remote(block, block, ys.at[k], yr.at[k], mid_peer).start()
+            remote(block, block, ys.at[0], yr.at[k], mid_peer).start()
         else:
             @pl.when(p > 0)
             def _():
-                remote(block, block, ys.at[k], yr.at[k], mid_peer).start()
+                remote(block, block, ys.at[0], yr.at[k], mid_peer).start()
 
         if relay:
             @pl.when(hop_of(p) == 2)
             def _():
-                remote(block, block, ws.at[h], zr.at[k], on_line(near)).start()
+                remote(block, block, ws.at[0], zr.at[k], on_line(near)).start()
 
     def send_core(i):
         h = i % HALVES
@@ -326,13 +327,28 @@
         k = unit * HALVES + h
         drain(qall.at[half(h), unit, c, 1 - b], yr.at[k])
         block = qall.at[half(h), unit, c]
-        remote(block, block, bs.at[k], br.at[k], core_peer).start()
+        remote(block, block, bs.at[0], br.at[k], core_peer).start()
 
     own_q.wait()
     if U > 1:
         for i in range(HALVES):
             send_middle(i)
 
+    side, place = me // (n // 2), me % (n // 2)
+
+    def send_rows(peer):
+        remote(rows_send.at[peer], rows_out.at[me], rs.at[0], rr.at[0], peer).start()
+
+    def far_rows():
+        @pl.loop(0, n // 2)
+        def _(k):
+            send_rows((1 - side) * (n // 2) + lax.rem(place + k, n // 2))
+
+    def near_rows():
+        @pl.loop(1, n // 2)
+        def _(k):
+            send_rows(side * (n // 2) + lax.rem(place + k, n // 2))
+
     @pl.loop(0, units + 1)
     def _(step):
         @pl.when(step == 0)
@@ -367,16 +383,18 @@
             drain(qall.at[half(h), unit, 1 - c], br.at[unit * HALVES + h])
             compute(unit, h)
 
+        @pl.when(step == FAR_STEP)
+        def _():
+            far_rows()
+
         @pl.when(step >= lag)
         def _():
             join_pair(step - lag)
 
     join_pair(units - 1)
 
-    @pl.loop(1, n)
-    def _(k):
-        peer = lax.rem(me + k, n)
-        remote(rows_send.at[peer], rows_out.at[me], rs.at[0], rr.at[0], peer).start()
+    near_rows()
+    far_rows()
 
     @pl.loop(0, units)
     def _(i):
@@ -450,21 +468,16 @@
     drain(rows_out.at[pl.ds(0, n - 1)], rr.at[0])
     drain(rows_send.at[pl.ds(0, n - 1)], rs.at[0])
 
-    @pl.loop(0, HALVES)
-    def _(h):
-        if relay:
-            drain(pieces(2), zs.at[h])
-            drain(pieces(1), ws.at[h])
-        else:
-            drain(pieces(A - 1), zs.at[h])
-
-    @pl.loop(0, units)
-    def _(k):
-        r, h = k // HALVES, k % HALVES
-        drain(qall.at[half(h), r, c, b], ys.at[k])
-        drain(qall.at[half(h), r, c], bs.at[k])
-        drain(stat_x.at[k, pl.ds(0, 1)], xs.at[k])
-        drain(stat_z.at[k, pl.ds(0, chips - 1)], qs.at[k])
+    if relay:
+        drain(pieces(2 * HALVES), zs.at[0])
+        drain(pieces(HALVES), ws.at[0])
+    else:
+        drain(pieces((A - 1) * HALVES), zs.at[0])
+
+    drain(pieces(units * U), ys.at[0])
+    drain(pieces(2 * units * U), bs.at[0])
+    drain(stat, xs.at[0])
+    drain(stat_z.at[:, pl.ds(0, chips - 1)], qs.at[0])
 
     @pl.when(me > 0)
     def _():
@@ -552,7 +565,7 @@
             pltpu.VMEM((slots,), jnp.int32),
             pltpu.VMEM((slots,), jnp.int32),
         ]
-        + [dma((units,))] * 12
+        + [dma((1,)), dma((units,))] * 6
         + [dma((1,)), dma((1,)), dma((2,)), dma((2,)), dma((1,)), dma((1,)), dma((7,))],
         compiler_params=pltpu.CompilerParams(
             collective_id=0, has_side_effects=True, vmem_limit_bytes=60 * 1024 * 1024

time: 44.1 us -> 42.5 us (0.964)
  Pallas kernels: 42.6 us -> 41.1 us
    pallas_call x1, Pallas kernels: 40.9 us -> 39.3 us  [per_device(): pl.pallas_call(functools.partial(kernel, n, cap, cap_pad, pool_scale), ou...]
where the time goes in v5:
time: 42.5 us; the launch traced here: 42.4 us
  Pallas kernels  41.1 us (97%)
  between operations  1.29 us (3%)
    pallas_call x1, Pallas kernels, per_device(): pl.pallas_call(functools.partial(kernel, n, cap, cap_pad, pool_scale), ou...  39.3 us
    pallas_call x1, Pallas kernels, per_device(): pl.pallas_call(functools.partial(finish, cap), out_shape=(jax.ShapeDtypeS...  1.76 us

profile of v5, /device:TPU:0, one launch (start us, length us, event | category | flops | bytes accessed | tf_op | source)
XLA Modules:
  0.0 42.4 jit_solution(16861191403952253356)
XLA Ops:
  1.3 39.3 %snap.1 = (f32[8,1024]{1,0:T(8,128)}, bf16[16,40,256]{2,1,0:T(8,128)(2,1)}, f32[16,1,128]{2,1,0:T(1,128)}) custom-call(bf16[1024,1024]{1,0:T(8,128)(2,1)} %keys_hbm.1, bf16[1024,1024]{1,0:T(8,128)(2,1)} %vals_hbm.1, bf16[8,64,128]{2,1,0:T(8,128)(2,1)} %bitcast.6, s32[1]{0:T(128)S(6)} %copy.9.count_hbm, s32[640]{0:T(1024)} %entry_hbm.1, s32[640]{0:T(1024)} %owner_hbm.1), custom_call_target="tpu_custom_call" | custom-call | tf_op jit(solution)/shard_map/snap/pallas_call | solution.py:535
  40.6 1.8 %finish.1 = (f32[8,1024]{1,0:T(8,128)}, bf16[16,40,256]{2,1,0:T(8,128)(2,1)}, bf16[640]{0:T(1024)(128)(2,1)}) custom-call(f32[8,1024]{1,0:T(8,128)} %get-tuple-element.9.imp_in, bf16[16,40,256]{2,1,0:T(8,128)(2,1)} %get-tuple-element.10.rows_in, f32[16,1,128]{2,1,0:T(1,128)} %get-tuple-element.11.score_in), custom_call_target="tpu_custom_call" | custom-call | tf_op jit(solution)/shard_map/finish/pallas_call | solution.py:575

commit v6 on v5

--- a/solution.py
+++ b/solution.py
@@ -16,7 +16,6 @@
 EDGE = 16
 STRIP = 64
 HALVES = 2
-FAR_STEP = -1
 MESH = pl.DeviceIdType.MESH
 NT = (((1,), (1,)), ((), ()))
 
@@ -138,30 +137,27 @@
     def on_line(index):
         return index * 4 + b * 2 + c
 
+    def send_own(h):
+        piece, place, k = wq_hbm.at[half(h)], qall.at[half(h), mine, c, b, inner], mine * HALVES + h
+        if U == 1:
+            remote(piece, place, ys.at[0], yr.at[k], mid_peer).start()
+
+        def send(index):
+            remote(piece, place, zs.at[0], zr.at[k], on_line(index)).start()
+
+        if relay:
+            send(near)
+            send(across)
+        else:
+            @pl.loop(1, A)
+            def _(i):
+                send(lax.rem(a + i, A))
+
     def greet():
         ends = jnp.where(me > 0, 1, 0) + jnp.where(me < n - 1, 1, 0)
         pl.semaphore_wait(barrier, A + 1 + ends)
 
-        if U == 1:
-            @pl.loop(0, HALVES)
-            def _(h):
-                k = mine * HALVES + h
-                remote(wq_hbm.at[half(h)], qall.at[half(h), mine, c, b, inner], ys.at[0], yr.at[k], mid_peer).start()
-
-        @pl.loop(0, HALVES)
-        def _(h):
-            piece, place, k = wq_hbm.at[half(h)], qall.at[half(h), mine, c, b, inner], mine * HALVES + h
-
-            def send(index):
-                remote(piece, place, zs.at[0], zr.at[k], on_line(index)).start()
-
-            if relay:
-                send(near)
-                send(across)
-            else:
-                @pl.loop(1, A)
-                def _(i):
-                    send(lax.rem(a + i, A))
+        send_own(0)
 
         @pl.when(me > 0)
         def _():
@@ -228,6 +224,10 @@
                 ].astype(jnp.bfloat16)
 
     per = onehot.shape[0] // cap_pad
+    @pl.when(reach >= A // 2)
+    def _():
+        send_own(1)
+
     gather_rows(0, per)
 
     @pl.when(reach < A // 2)
@@ -330,6 +330,11 @@
         remote(block, block, bs.at[0], br.at[k], core_peer).start()
 
     own_q.wait()
+
+    @pl.when(reach < A // 2)
+    def _():
+        send_own(1)
+
     if U > 1:
         for i in range(HALVES):
             send_middle(i)
@@ -382,10 +387,6 @@
             unit = unit_at((step - 1) // HALVES)
             drain(qall.at[half(h), unit, 1 - c], br.at[unit * HALVES + h])
             compute(unit, h)
-
-        @pl.when(step == FAR_STEP)
-        def _():
-            far_rows()
 
         @pl.when(step >= lag)
         def _():

time: 42.5 us -> 42 us (0.988)
  Pallas kernels: 41.1 us -> 40.5 us
    pallas_call x1, Pallas kernels: 39.3 us -> 38.8 us  [per_device(): pl.pallas_call(functools.partial(kernel, n, cap, cap_pad, pool_scale), ou...]
where the time goes in v6:
time: 42 us; the launch traced here: 41.8 us
  Pallas kernels  40.5 us (96%)
  between operations  1.29 us (3%)
    pallas_call x1, Pallas kernels, per_device(): pl.pallas_call(functools.partial(kernel, n, cap, cap_pad, pool_scale), ou...  38.8 us
    pallas_call x1, Pallas kernels, per_device(): pl.pallas_call(functools.partial(finish, cap), out_shape=(jax.ShapeDtypeS...  1.76 us

profile of v6, /device:TPU:0, one launch (start us, length us, event | category | flops | bytes accessed | tf_op | source)
XLA Modules:
  0.0 41.8 jit_solution(15761099148001973548)
XLA Ops:
  1.3 38.8 %snap.1 = (f32[8,1024]{1,0:T(8,128)}, bf16[16,40,256]{2,1,0:T(8,128)(2,1)}, f32[16,1,128]{2,1,0:T(1,128)}) custom-call(bf16[1024,1024]{1,0:T(8,128)(2,1)} %keys_hbm.1, bf16[1024,1024]{1,0:T(8,128)(2,1)} %vals_hbm.1, bf16[8,64,128]{2,1,0:T(8,128)(2,1)} %bitcast.6, s32[1]{0:T(128)S(6)} %copy.9.count_hbm, s32[640]{0:T(1024)} %entry_hbm.1, s32[640]{0:T(1024)} %owner_hbm.1), custom_call_target="tpu_custom_call" | custom-call | tf_op jit(solution)/shard_map/snap/pallas_call | solution.py:536
  40.0 1.8 %finish.1 = (f32[8,1024]{1,0:T(8,128)}, bf16[16,40,256]{2,1,0:T(8,128)(2,1)}, bf16[640]{0:T(1024)(128)(2,1)}) custom-call(f32[8,1024]{1,0:T(8,128)} %get-tuple-element.9.imp_in, bf16[16,40,256]{2,1,0:T(8,128)(2,1)} %get-tuple-element.10.rows_in, f32[16,1,128]{2,1,0:T(1,128)} %get-tuple-element.11.score_in), custom_call_target="tpu_custom_call" | custom-call | tf_op jit(solution)/shard_map/finish/pallas_call | solution.py:576

commit v7 on v6

--- a/solution.py
+++ b/solution.py
@@ -146,8 +146,8 @@
             remote(piece, place, zs.at[0], zr.at[k], on_line(index)).start()
 
         if relay:
-            send(near)
-            send(across)
+            send(jnp.where(a < 2, across, near))
+            send(jnp.where(a < 2, near, across))
         else:
             @pl.loop(1, A)
             def _(i):

time: 42 us -> 41.9 us (level)
  no operation moved by 1% of the time
where the time goes in v7:
time: 41.9 us; the launch traced here: 41.7 us
  Pallas kernels  40.4 us (96%)
  between operations  1.29 us (3%)
    pallas_call x1, Pallas kernels, per_device(): pl.pallas_call(functools.partial(kernel, n, cap, cap_pad, pool_scale), ou...  38.7 us
    pallas_call x1, Pallas kernels, per_device(): pl.pallas_call(functools.partial(finish, cap), out_shape=(jax.ShapeDtypeS...  1.76 us

profile of v7, /device:TPU:0, one launch (start us, length us, event | category | flops | bytes accessed | tf_op | source)
XLA Modules:
  0.0 41.7 jit_solution(3537249444212000242)
XLA Ops:
  1.3 38.7 %snap.1 = (f32[8,1024]{1,0:T(8,128)}, bf16[16,40,256]{2,1,0:T(8,128)(2,1)}, f32[16,1,128]{2,1,0:T(1,128)}) custom-call(bf16[1024,1024]{1,0:T(8,128)(2,1)} %keys_hbm.1, bf16[1024,1024]{1,0:T(8,128)(2,1)} %vals_hbm.1, bf16[8,64,128]{2,1,0:T(8,128)(2,1)} %bitcast.6, s32[1]{0:T(128)S(6)} %copy.9.count_hbm, s32[640]{0:T(1024)} %entry_hbm.1, s32[640]{0:T(1024)} %owner_hbm.1), custom_call_target="tpu_custom_call" | custom-call | tf_op jit(solution)/shard_map/snap/pallas_call | solution.py:536
  39.9 1.8 %finish.1 = (f32[8,1024]{1,0:T(8,128)}, bf16[16,40,256]{2,1,0:T(8,128)(2,1)}, bf16[640]{0:T(1024)(128)(2,1)}) custom-call(f32[8,1024]{1,0:T(8,128)} %get-tuple-element.9.imp_in, bf16[16,40,256]{2,1,0:T(8,128)(2,1)} %get-tuple-element.10.rows_in, f32[16,1,128]{2,1,0:T(1,128)} %get-tuple-element.11.score_in), custom_call_target="tpu_custom_call" | custom-call | tf_op jit(solution)/shard_map/finish/pallas_call | solution.py:576
